TPU v7x, 32 devices: a whole 2x2x4 slice. The times are simulated.
32 devices in a mesh: occ: 2 (over core), vir: 16 (over z, y, x).
Axes of the slice: x: 2, y: 2, z: 4, core: 2. Of those that a mesh axis runs over, the one named last changes fastest.
Arguments:
- amplitudes: bfloat16 [2256, 6144], P('occ', 'vir'), may hold values from -6 to 6
- ladder_ints: bfloat16 [6144, 6144], P('vir', 'occ'), as said below
- tile_map: int32 [48, 48], replicated, may hold values from 0 to 1, as said below
- hole_ints: bfloat16 [2256, 2256], P('occ'), may hold values from -0.125 to 0.125
- occ_energy: float32 [48], replicated, may hold values from -2 to -0.3
- pair_list: int32 [2256, 2], P('occ'), may hold values from 0 to 47, as said below
- mirror_row: int32 [2256], P('occ'), may hold values from 0 to 2255, as said below
Outputs:
- residual: float32 [2256, 6144], P('occ', 'vir')
Inputs may be any that keep to these rules, and one draw needn't show every extreme that they name: symmetric: ladder_ints[ab, cd] equals ladder_ints[cd, ab]. `tile_map`: symmetric. `pair_list`: each ordered pair of distinct orbitals of the 48 occupied ones stands in exactly one row. Row mirror_row[r] holds the pair of row r reversed.
All inputs are finite; a program needn't handle non-finite values.
Results may differ from a plain program's by a relative error of at most 0.0003.
Values may be sent and summed in bfloat16 or wider, within the bound.
No kernel may reach another device: no remote copies, remote signals or barrier semaphores. Data moves between devices by JAX's collectives and lax.ppermute only.
A program may use at most 64 MiB of HBM per device.

v0:
```python
import jax
import jax.numpy as jnp
from jax import lax
from jax.sharding import PartitionSpec as P

TILE = 128


def shards(amplitudes, ladder_ints, tile_map, hole_ints, occ_energy, pair_list, mirror_row):
    local_rows, local_cols = amplitudes.shape
    integral_cols = ladder_ints.shape[1]
    vir_place = lax.axis_index("vir")
    occ_place = lax.axis_index("occ")
    row_tiles = local_cols // TILE
    col_tiles = integral_cols // TILE
    tile_block = lax.dynamic_slice(
        tile_map, (vir_place * row_tiles, occ_place * col_tiles), (row_tiles, col_tiles)
    )
    tile_mask = jnp.broadcast_to(tile_block[:, None, :, None], (row_tiles, TILE, col_tiles, TILE))
    masked = ladder_ints * tile_mask.reshape(local_cols, integral_cols).astype(ladder_ints.dtype)
    whole_amps = lax.all_gather(amplitudes, "vir", axis=1, tiled=True)
    ladder = lax.dot_general(
        whole_amps,
        lax.all_gather(masked, "occ", axis=1, tiled=True),
        (((1,), (1,)), ((), ())),
        preferred_element_type=jnp.float32,
    )
    hole = jnp.dot(
        hole_ints,
        lax.all_gather(amplitudes, "occ", axis=0, tiled=True),
        preferred_element_type=jnp.float32,
    )
    orbital_ids = jnp.arange(occ_energy.shape[0], dtype=jnp.int32)
    one_hot = (pair_list[:, :, None] == orbital_ids[None, None, :]).astype(jnp.float32)
    pair_energy = jnp.sum(one_hot * occ_energy[None, None, :], axis=(1, 2))
    raw = ladder + hole - pair_energy[:, None] * amplitudes.astype(jnp.float32)
    all_raw = lax.all_gather(raw, "occ", axis=0, tiled=True)
    mirrored = jnp.take(all_raw, mirror_row, axis=0)
    swapped = mirrored.reshape(local_rows, local_cols // 2, 2)[:, :, ::-1].reshape(
        local_rows, local_cols
    )
    return raw + swapped


def solution(mesh):
    return jax.shard_map(
        shards,
        mesh=mesh,
        in_specs=(
            P("occ", "vir"),
            P("vir", "occ"),
            P(),
            P("occ", None),
            P(),
            P("occ", None),
            P("occ"),
        ),
        out_specs=P("occ", "vir"),
        check_vma=False,
    )
```

profile of v0, /device:TPU:0, one launch (start us, length us, event | category | flops | bytes accessed | tf_op | source)
XLA Modules:
  0.0 254.0 jit_solution(10276465608490129441)
XLA Ops:
  6.5 0.0 copy-start.2
  6.5 0.0 all-gather.5.cloned.1.call-start
  6.5 0.9 dynamic-slice_convert_fusion
  7.5 0.4 broadcast_in_dim.22
  7.8 0.4 copy-done.2
  8.2 1.7 bitcast_multiply_fusion
  9.9 0.0 copy-start.4
  9.9 0.0 copy-start.5
  9.9 0.0 all-gather.5.cloned.1.call-update
  9.9 0.0 all-gather.7.cloned.1.call-start
  10.0 0.7 all-gather.7.cloned.1.call-update
  10.7 0.0 all-gather.9.cloned.1.call-start
  10.7 0.7 all-gather.9.cloned.1.call-update
  11.4 0.0 all-gather.11.cloned.1.call-start
  11.5 0.0 copy-done.4
  11.5 0.0 copy-done.5
  11.5 0.1 select_reduce_fusion
  11.6 0.0 copy-start.1
  11.6 15.6 %all-gather.5.cloned.1.call-done = bf16[384,6144]{1,0:T(8,128)(2,1)} async-done(((bf16[384,3072]{1,0:T(8,128)(2,1)}), bf16[384,6144]{1,0:T(8,128)(2,1)}) %all-gather.5.cloned.1.call-update) | async-done | bytes 4718608 | tf_op jit(solution)/shard_map/all_gather | solution.py:24
  27.3 168.0 %all-gather.7.cloned.1.call-done = bf16[1128,6144]{1,0:T(8,128)(2,1)} async-done(((bf16[1128,384]{1,0:T(8,128)(2,1)}), bf16[1128,6144]{1,0:T(8,128)(2,1)}) %all-gather.7.cloned.1.call-update) | async-done | bytes 13860880 | tf_op jit(solution)/shard_map/all_gather | solution.py:21
  195.2 11.7 %convolution_bitcast_fusion = f32[1128,384]{1,0:T(8,128)S(1)} fusion(bf16[384,6144]{1,0:T(8,128)(2,1)} %all-gather.5.cloned.1.call-done, bf16[1128,6144]{1,0:T(8,128)(2,1)} %all-gather.7.cloned.1.call-done), kind=kOutput, calls=%fused_computation.3 | convolution fusion | flops 5322571776 | bytes 20312064 | tf_op jit(solution)/shard_map/dot_general | solution.py:22
  207.0 0.0 copy-start.3
  207.0 0.0 all-gather.9.cloned.1.call-done
  207.0 0.0 copy-done.1
  207.0 7.2 %fusion = f32[1128,384]{1,0:T(8,128)} fusion(f32[1128,384]{1,0:T(8,128)S(1)} %convolution_bitcast_fusion, bf16[1128,2256]{1,0:T(8,128)(2,1)} %param.10, bf16[2256,384]{1,0:T(8,128)(2,1)} %all-gather.9.cloned.1.call-done, bf16[1128,384]{1,0:T(8,128)(2,1)S(1)} %copy-done.1, f32[1128]{0:T(1024)S(1)} %select_reduce_fusion), kind=kOutput, calls=%fused_computation.2 | convolution fusion | flops 1956114432 | bytes 11158176 | tf_op jit(solution)/shard_map/dot_general | solution.py:28
  214.2 0.0 all-gather.11.cloned.1.call-update
  214.2 0.0 copy-done.3
  214.3 11.9 %all-gather.11.cloned.1.call-done = f32[2256,384]{1,0:T(8,128)} async-done(((f32[1128,384]{1,0:T(8,128)}), f32[2256,384]{1,0:T(8,128)}) %all-gather.11.cloned.1.call-update) | async-done | bytes 3465232 | tf_op jit(solution)/shard_map/all_gather | solution.py:37
  226.2 6.0 %gather_fusion = f32[1128,384]{1,0:T(8,128)S(1)} fusion(f32[2256,384]{1,0:T(8,128)} %all-gather.11.cloned.1.call-done, s32[2048]{0:T(1024)S(1)} %pad_clamp_fusion), kind=kCustom, calls=%fused_computation | custom fusion | bytes 3469728 | tf_op jit(solution)/shard_map/jit(_take)/gather | solution.py:38
  232.2 1.2 copy.12
  233.4 1.1 gather.7
  234.4 0.8 broadcast_select_fusion
  235.2 6.4 %rev.3 = f32[1128,192,2]{0,2,1:T(2,128)S(1)} reverse(f32[1128,192,2]{0,2,1:T(2,128)S(1)} %broadcast_select_fusion), dimensions={2} | reverse | bytes 3465216 | tf_op jit(solution)/shard_map/rev | solution.py:39
  241.6 1.2 reshape.21
  242.8 0.0 copy-start
  242.8 1.8 copy.13
  244.6 0.0 copy-done
  244.6 2.8 %add.25 = f32[1128,384]{1,0:T(8,128)} add(f32[1128,384]{1,0:T(8,128)S(1)} %copy-done, f32[1128,384]{1,0:T(8,128)} %copy.13) | non-fusion elementwise | flops 433152 | bytes 5197824 | tf_op jit(solution)/shard_map/add | solution.py:42
  (3 shorter events, 0.0 us)
Async XLA Ops:
  6.5 1.7 copy-start.2
  6.5 20.7 %all-gather.5.cloned.1.call-start = ((), (), s32[]{:S(2)}) async-start(), calls=%async_computation | async-start | bytes 7077888 | tf_op jit(solution)/shard_map/all_gather | solution.py:24
  9.9 1.6 copy-start.4
  9.9 1.6 copy-start.5
  9.9 185.3 %all-gather.7.cloned.1.call-start = ((), (), s32[]{:S(2)}) async-start(), calls=%async_computation.1 | async-start | bytes 14727168 | tf_op jit(solution)/shard_map/all_gather | solution.py:21
  10.7 196.3 %all-gather.9.cloned.1.call-start = ((), (), s32[]{:S(2)}) async-start(), calls=%async_computation.2 | async-start | bytes 2598912 | tf_op jit(solution)/shard_map/all_gather | solution.py:30
  11.4 214.7 %all-gather.11.cloned.1.call-start = ((), (), s32[]{:S(2)}) async-start(), calls=%async_computation.3 | async-start | bytes 5197824 | tf_op jit(solution)/shard_map/all_gather | solution.py:37
  11.6 195.4 %copy-start.1 = (bf16[1128,384]{1,0:T(8,128)(2,1)S(1)}, bf16[1128,384]{1,0:T(8,128)(2,1)}, u32[]{:S(2)}) copy-start(bf16[1128,384]{1,0:T(8,128)(2,1)} %param.7) | copy-start | bytes 2598916
  207.0 7.3 %copy-start.3 = (s32[1128]{0:T(1024)S(1)}, s32[1128]{0:T(1024)}, u32[]{:S(2)}) copy-start(s32[1128]{0:T(1024)} %param.13) | copy-start | bytes 13540
  242.8 1.8 copy-start
Sparse Core Ops, SparseCore 0:
  10.1 17.1 all-gather.4
  30.0 165.2 all-gather.6
  196.8 8.2 all-gather.8
  214.3 11.7 all-gather.10
where the time goes:
time: 254 us
  waiting for transfers between devices  197 us (78%)
  matrix products  18.9 us (7%)
  local copies, waits for them, and re-layouts  18.4 us (7%)
  between operations  13.3 us (5%)
  other arithmetic  6.38 us (3%)
    all_gather x1, waiting for transfers between devices, shards(): whole_amps = lax.all_gather(amplitudes, 'vir', axis=1, tiled=True)  168 us
    all_gather x1, waiting for transfers between devices, shards(): lax.all_gather(masked, 'occ', axis=1, tiled=True)  15.6 us
    all_gather x1, waiting for transfers between devices, shards(): all_raw = lax.all_gather(raw, 'occ', axis=0, tiled=True)  11.9 us
    dot_general x1, matrix products, shards(): lax.dot_general(whole_amps, lax.all_gather(masked, 'occ', axis=1, tiled=T...  11.7 us
    gather x3, local copies, waits for them, and re-layouts, shards(): mirrored = jnp.take(all_raw, mirror_row, axis=0)  8.22 us
    dot_general x1, matrix products, shards(): jnp.dot(hole_ints, lax.all_gather(amplitudes, 'occ', axis=0, tiled=True),...  7.19 us
    rev x1, local copies, waits for them, and re-layouts, shards(): mirrored.reshape(local_rows, local_cols // 2, 2)[:, :, ::-1]  6.4 us
  transfers between devices with their start and end apart: 4, of which 3 were waited for; matrix products, arithmetic and copies ran while one was open for 5% of the time, Pallas kernels for 0%

commit v1 on v0

v1 whole, which is shorter than its diff:
```python
import functools

import jax
import jax.numpy as jnp
from jax import lax
from jax.experimental import pallas as pl
from jax.experimental.pallas import tpu as pltpu
from jax.sharding import PartitionSpec as P


TILE = 128
CHUNKS = 4


LIMIT = 16 * 1024 * 1024

SMEM = pl.BlockSpec(memory_space=pltpu.SMEM)
VMEM = pl.BlockSpec(memory_space=pltpu.VMEM)
ANY = pl.BlockSpec(memory_space=pl.ANY)


def row_chunks(rows, count):
    step = -(-rows // (count * 8)) * 8
    starts = list(range(0, rows, step))
    return [(start, min(step, rows - start)) for start in starts]


def other_core(a):
    return lax.ppermute(a, "occ", [(0, 1), (1, 0)])


def rows_kernel(chunks, a_ref, *refs):
    for (start, length), out in zip(chunks, refs):
        out[...] = a_ref[start : start + length, :]


def split_rows(a, chunks):
    return pl.pallas_call(
        functools.partial(rows_kernel, chunks),
        out_shape=[jax.ShapeDtypeStruct((length, a.shape[1]), a.dtype) for _, length in chunks],
        in_specs=[VMEM],
        out_specs=[VMEM] * len(chunks),
        compiler_params=pltpu.CompilerParams(vmem_limit_bytes=LIMIT),
        cost_estimate=pl.CostEstimate(flops=0, bytes_accessed=2 * a.size * 2, transcendentals=0),
        name="split_rows",
    )(a)


def sides_kernel(where_ref, map_ref, v_ref, send_ref, kept_ref):
    side, first_row, first_col = where_ref[0], where_ref[1], where_ref[2]
    cols = v_ref.shape[0]
    tiles = cols // TILE
    for out, which in ((send_ref, 1 - side), (kept_ref, side)):
        for j in range(out.shape[1] // cols):
            block = 2 * j + which
            for r in range(tiles):
                for c in range(tiles):
                    allowed = map_ref[first_row + r, first_col + block * tiles + c]
                    at = pl.multiple_of(block * cols + c * TILE, TILE)
                    tile = v_ref[r * TILE : (r + 1) * TILE, pl.ds(at, TILE)]
                    out[r * TILE : (r + 1) * TILE, j * cols + c * TILE : j * cols + (c + 1) * TILE] = (
                        jnp.where(allowed == 1, tile, jnp.zeros_like(tile))
                    )


def split_sides(where, tile_map, integrals):
    cols, width = integrals.shape
    half = jax.ShapeDtypeStruct((cols, width // 2), integrals.dtype)
    return pl.pallas_call(
        sides_kernel,
        out_shape=[half, half],
        in_specs=[SMEM, SMEM, VMEM],
        out_specs=[VMEM, VMEM],
        compiler_params=pltpu.CompilerParams(vmem_limit_bytes=LIMIT),
        cost_estimate=pl.CostEstimate(
            flops=integrals.size, bytes_accessed=4 * integrals.size, transcendentals=0
        ),
        name="split_sides",
    )(where, tile_map, integrals)


def product_kernel(count, parts, start, at_ref, *refs):
    blocks, pieces = refs[:count], refs[count : count + parts]
    addend = refs[count + parts] if start is not None else None
    out_ref, piece_buf, sems = refs[-3:]
    length, cols = out_ref.shape
    per_piece = pieces[0].shape[1] // cols

    def piece_copy(k, p, at):
        return pltpu.make_async_copy(
            pieces[p].at[:, pl.ds(pl.multiple_of(at * cols, cols), cols)], piece_buf.at[k], sems.at[k]
        )

    for k in range(count):
        for p in range(parts):
            at = at_ref[k] - p * per_piece

            @pl.when((at >= 0) & (at < per_piece))
            def _():
                piece_copy(k, p, at).start()

    for k in range(count):
        piece_copy(k, 0, 0).wait()
        term = lax.dot_general(
            blocks[k][...], piece_buf[k], (((1,), (1,)), ((), ())), preferred_element_type=jnp.float32
        )
        if k > 0:
            out_ref[...] += term
        elif start is not None:
            out_ref[...] = term + addend[start : start + length, :]
        else:
            out_ref[...] = term


def product(at, blocks, pieces, addend=None, start=None):
    count, parts = len(blocks), len(pieces)
    length, cols = blocks[0].shape
    given = [addend] if start is not None else []
    return pl.pallas_call(
        functools.partial(product_kernel, count, parts, start),
        out_shape=jax.ShapeDtypeStruct((length, cols), jnp.float32),
        in_specs=[SMEM] + [VMEM] * (count + parts + len(given)),
        out_specs=VMEM,
        scratch_shapes=[
            pltpu.VMEM((count, cols, cols), jnp.bfloat16),
            pltpu.SemaphoreType.DMA((count,)),
        ],
        compiler_params=pltpu.CompilerParams(vmem_limit_bytes=LIMIT),
        cost_estimate=pl.CostEstimate(
            flops=2 * count * length * cols * cols,
            bytes_accessed=2 * count * (length + cols) * cols + 4 * length * cols,
            transcendentals=0,
        ),
        name="product",
    )(at, *blocks, *pieces, *given)


def mirror_kernel(offsets, index_ref, *refs):
    *pieces, out_ref, whole, sems = refs
    copies = []
    for k, offset in enumerate(offsets):
        copy = pltpu.make_async_copy(
            pieces[k], whole.at[pl.ds(offset, pieces[k].shape[0])], sems.at[k]
        )
        copy.start()
        copies.append(copy)
    for copy in copies:
        copy.wait()
    rows, cols = out_ref.shape
    odd = lax.broadcasted_iota(jnp.int32, (8, TILE), 1) % 2 == 1

    def group(start, size):
        picked = jnp.concatenate(
            [whole[pl.ds(index_ref[start + j], 1), :] for j in range(size)], axis=0
        )
        for c in range(0, cols, TILE):
            part = picked[:, c : c + TILE]
            swapped = jnp.where(odd[:size], pltpu.roll(part, 1, 1), pltpu.roll(part, TILE - 1, 1))
            out_ref[pl.ds(start, size), c : c + TILE] = (
                whole[pl.ds(start, size), c : c + TILE] + swapped
            )

    def step(g, carry):
        group(pl.multiple_of(g * 8, 8), 8)
        return carry

    lax.fori_loop(0, rows // 8, step, 0)
    if rows % 8:
        group(rows // 8 * 8, rows % 8)


def add_mirror(index, rows, pieces):
    cols = pieces[0].shape[1]
    offsets, total = [], 0
    for piece in pieces:
        offsets.append(total)
        total += -(-piece.shape[0] // 8) * 8
    return pl.pallas_call(
        functools.partial(mirror_kernel, tuple(offsets)),
        out_shape=jax.ShapeDtypeStruct((rows, cols), jnp.float32),
        in_specs=[SMEM] + [ANY] * len(pieces),
        out_specs=VMEM,
        scratch_shapes=[
            pltpu.VMEM((total, cols), jnp.float32),
            pltpu.SemaphoreType.DMA((len(pieces),)),
        ],
        compiler_params=pltpu.CompilerParams(vmem_limit_bytes=LIMIT),
        cost_estimate=pl.CostEstimate(
            flops=rows * cols, bytes_accessed=(total + rows) * cols * 4, transcendentals=0
        ),
        name="mirror",
    )(index, *pieces)


def shards(cores, chips, amplitudes, ladder_ints, tile_map, hole_ints, occ_energy, pair_list, mirror_row):
    rows, cols = amplitudes.shape
    integral_cols = ladder_ints.shape[1]
    vir_place = lax.axis_index("vir")
    occ_place = lax.axis_index("occ")
    members = chips // 2
    half_blocks = integral_cols // cols // 2
    side = vir_place % 2
    group = vir_place // 2
    across = [(v, v ^ 1) for v in range(chips)]

    evens = (members + 1) // 2
    order = [2 * p if p < evens else 2 * (members - p) - 1 for p in range(members)]
    forward, backward = [], []
    for s in range(2):
        for k in range(members):
            here, there = 2 * order[k] + s, 2 * order[(k + 1) % members] + s
            forward.append((here, there))
            backward.append((there, here))
    place = jnp.where(group % 2 == 0, group // 2, members - (group + 1) // 2)
    own_half = occ_place * half_blocks if cores == 2 else 0

    def positions(steps):
        p = (place - jnp.array(steps, jnp.int32)) % members
        g = jnp.where(p < evens, 2 * p, 2 * (members - p) - 1)
        return (g - own_half) % members

    def whole_k(a):
        if cores == 2:
            return [a, other_core(a)]
        return [lax.all_gather(a, "occ", axis=1, tiled=True)]

    chunks = row_chunks(rows, CHUNKS)
    mine = split_rows(amplitudes, chunks)

    where = jnp.stack([side, vir_place * (cols // TILE), occ_place * (integral_cols // TILE)])
    send, kept = split_sides(where.astype(jnp.int32), tile_map, ladder_ints)
    near = lax.ppermute(send, "vir", across)
    kept_all = whole_k(kept)
    near_all = whole_k(near)

    if cores == 2:
        both = jnp.zeros((2 * rows, cols), amplitudes.dtype)
        both = lax.dynamic_update_slice(both, amplitudes, (occ_place * rows, 0))
        both = lax.dynamic_update_slice(both, other_core(amplitudes), ((1 - occ_place) * rows, 0))
    else:
        both = lax.all_gather(amplitudes, "occ", axis=0, tiled=True)
    orbital_ids = jnp.arange(occ_energy.shape[0], dtype=jnp.int32)
    one_hot = (pair_list[:, :, None] == orbital_ids[None, None, :]).astype(jnp.float32)
    pair_energy = jnp.sum(one_hot * occ_energy[None, None, :], axis=(1, 2))
    base = jnp.dot(hole_ints, both, preferred_element_type=jnp.float32)
    base = base - pair_energy[:, None] * amplitudes.astype(jnp.float32)

    raws = []
    for index, (start, length) in enumerate(chunks):
        ups = members // 2 if index % 2 == 0 else (members - 1) // 2
        blocks = {0: mine[index]}
        for step in range(1, ups + 1):
            blocks[step] = lax.ppermute(blocks[step - 1], "vir", forward)
        for step in range(1, members - ups):
            blocks[-step] = lax.ppermute(blocks[1 - step], "vir", backward)
        steps = sorted(blocks, key=abs)
        at = positions(steps)
        arrived = [blocks[s] for s in steps]
        for_near = product(at, arrived, near_all)
        from_near = lax.ppermute(for_near, "vir", across)
        rest = product(at, arrived, kept_all, base, start)
        raws.append(rest + from_near)

    if cores == 2:
        pieces = raws + [other_core(raw) for raw in raws]
        index = (mirror_row - occ_place * rows) % (2 * rows)
        return add_mirror(index, rows, pieces)
    own = jnp.concatenate(raws, axis=0)
    whole = lax.all_gather(own, "occ", axis=0, tiled=True)
    padded = -(-rows // 8) * 8
    own = jnp.pad(own, ((0, padded - rows), (0, 0)))
    return add_mirror(mirror_row + padded, rows, [own, whole])


def solution(mesh):
    cores, chips = mesh.shape["occ"], mesh.shape["vir"]

    def body(*arrays):
        return shards(cores, chips, *arrays)

    return jax.shard_map(
        body,
        mesh=mesh,
        in_specs=(
            P("occ", "vir"),
            P("vir", "occ"),
            P(),
            P("occ", None),
            P(),
            P("occ", None),
            P("occ"),
        ),
        out_specs=P("occ", "vir"),
        check_vma=False,
    )
```

time: 254 us -> 150 us (0.59)
  waiting for transfers between devices: 197 us -> 43.7 us
  Pallas kernels: 0 us -> 47.5 us
  starting transfers between devices: 0.12 us -> 41.4 us
  matrix products: 18.9 us -> 4 us
  between operations: 13.3 us -> 0.63 us
  local copies, waits for them, and re-layouts: 18.4 us -> 11.6 us
  other arithmetic: 6.38 us -> 0.49 us
    all_gather x4 -> x0, waiting for transfers between devices: 196 us -> none  [the longest x1 168 us: shards(): whole_amps = lax.all_gather(amplitudes, 'vir', axis=1, tiled=True)]
    pallas_call x0 -> x11, Pallas kernels: none -> 47.5 us  [the longest x8 28.8 us: product(): pl.pallas_call(functools.partial(product_kernel, count, parts, start), ou...]
    ppermute x0 -> x40, waiting for transfers between devices: none -> 43.7 us  [the longest x14 21.7 us: shards(): blocks[step] = lax.ppermute(blocks[step - 1], 'vir', forward)]
    ppermute x0 -> x40, starting transfers between devices: none -> 41.4 us  [the longest x14 19.7 us: shards(): blocks[step] = lax.ppermute(blocks[step - 1], 'vir', forward)]
    dot_general x2 -> x1, matrix products: 18.9 us -> 4 us  [shards(): base = jnp.dot(hole_ints, both, preferred_element_type=jnp.float32)]
    unnamed x12 -> x70, local copies, waits for them, and re-layouts: 0.4 us -> 8.7 us
    gather x3 -> x0, local copies, waits for them, and re-layouts: 8.22 us -> none  [shards(): mirrored = jnp.take(all_raw, mirror_row, axis=0)]
    rev x1 -> x0, local copies, waits for them, and re-layouts: 6.4 us -> none  [shards(): mirrored.reshape(local_rows, local_cols // 2, 2)[:, :, ::-1]]
  transfers between devices with their start and end apart: 4 -> 40, of which waited for: 3 -> 15; matrix products, arithmetic and copies ran while one was open for 5% -> 5% of each run, Pallas kernels for 0% -> 20%
where the time goes in v1:
time: 150 us; the launch traced here: 149 us
  Pallas kernels  47.5 us (32%)
  waiting for transfers between devices  43.7 us (29%)
  starting transfers between devices  41.4 us (28%)
  local copies, waits for them, and re-layouts  11.6 us (8%)
  matrix products  4 us (3%)
    pallas_call x8, Pallas kernels, product(): pl.pallas_call(functools.partial(product_kernel, count, parts, start), ou...  28.8 us
    ppermute x14, waiting for transfers between devices, shards(): blocks[step] = lax.ppermute(blocks[step - 1], 'vir', forward)  21.7 us
    ppermute x14, starting transfers between devices, shards(): blocks[step] = lax.ppermute(blocks[step - 1], 'vir', forward)  19.7 us
    pallas_call x1, Pallas kernels, add_mirror(): pl.pallas_call(functools.partial(mirror_kernel, tuple(offsets)), out_shap...  15.9 us
    ppermute x14, starting transfers between devices, shards(): blocks[-step] = lax.ppermute(blocks[1 - step], 'vir', backward)  13.7 us
    unnamed x70, local copies, waits for them, and re-layouts  8.7 us
    ppermute x1, waiting for transfers between devices, shards(): near = lax.ppermute(send, 'vir', across)  8 us
    ppermute x4, waiting for transfers between devices, shards(): from_near = lax.ppermute(for_near, 'vir', across)  7.52 us
  transfers between devices with their start and end apart: 40, of which 15 were waited for; matrix products, arithmetic and copies ran while one was open for 5% of the time, Pallas kernels for 20%

profile of v1, /device:TPU:0, one launch (start us, length us, event | category | flops | bytes accessed | tf_op | source)
XLA Modules:
  0.0 149.3 jit_solution(6433551925136164483)
XLA Ops:
  0.1 1.7 %copy-done = bf16[384,3072]{1,0:T(8,128)(2,1)S(1)} copy-done((bf16[384,3072]{1,0:T(8,128)(2,1)S(1)}, bf16[384,3072]{1,0:T(8,128)(2,1)}, u32[]{:S(2)}) %copy-start) | copy-done | bytes 2359320
  2.5 1.6 %split_sides.1 = (bf16[384,1536]{1,0:T(8,128)(2,1)S(1)}, bf16[384,1536]{1,0:T(8,128)(2,1)S(1)}) custom-call(s32[3]{0:T(128)S(1)} %pad_add_fusion.where_ref, s32[48,48]{1,0:T(8,128)S(1)} %copy-done.27, bf16[384,3072]{1,0:T(8,128)(2,1)S(1)} %copy-done), custom_call_target="tpu_custom_call" | custom-call | flops 1179648 | bytes 4718592 | tf_op jit(solution)/shard_map/split_sides/pallas_call | solution.py:69
  4.1 3.0 %collective-permute-start.9 = (bf16[384,1536]{1,0:T(8,128)(2,1)S(1)}, bf16[384,1536]{1,0:T(8,128)(2,1)S(1)}, u32[]{:S(2)}, u32[]{:S(2)}) collective-permute-start(bf16[384,1536]{1,0:T(8,128)(2,1)S(1)} %get-tuple-element.13), channel_id=1, source_target_pairs={{0,1},{1,0},{2,3},{3,2},{4,5},{5,4},{6,7},{7,6},{8,9},{9,8},{10,11... | collective-permute-start | bytes 3538952 | tf_op jit(solution)/shard_map/ppermute | solution.py:232
  7.1 1.2 split_rows.1
  8.3 1.6 %collective-permute-start = (bf16[288,384]{1,0:T(8,128)(2,1)S(1)}, bf16[288,384]{1,0:T(8,128)(2,1)S(1)}, u32[]{:S(2)}, u32[]{:S(2)}) collective-permute-start(bf16[288,384]{1,0:T(8,128)(2,1)S(1)} %get-tuple-element.11.refs_0_), channel_id=1, source_target_pairs={{0,4},{4,8},{8,12},{12,14},{14,10},{10,6},{6,2},{2,0},{1,5},{5,9},... | collective-permute-start | bytes 663560 | tf_op jit(solution)/shard_map/ppermute | solution.py:253
  10.0 1.6 %collective-permute-start.28 = (bf16[264,384]{1,0:T(8,128)(2,1)S(1)}, bf16[264,384]{1,0:T(8,128)(2,1)S(1)}, u32[]{:S(2)}, u32[]{:S(2)}) collective-permute-start(bf16[264,384]{1,0:T(8,128)(2,1)S(1)} %get-tuple-element.16.refs_0_), channel_id=1, source_target_pairs={{0,4},{4,8},{8,12},{12,14},{14,10},{10,6},{6,2},{2,0},{1,5},{5,9},... | collective-permute-start | bytes 608264 | tf_op jit(solution)/shard_map/ppermute | solution.py:253
  13.8 5.8 %collective-permute-done.28.refs_1_ = bf16[264,384]{1,0:T(8,128)(2,1)S(1)} collective-permute-done((bf16[264,384]{1,0:T(8,128)(2,1)S(1)}, bf16[264,384]{1,0:T(8,128)(2,1)S(1)}, u32[]{:S(2)}, u32[]{:S(2)}) %collective-permute-start.28) | collective-permute-done | bytes 202784 | tf_op jit(solution)/shard_map/ppermute | solution.py:253
  19.6 1.6 %collective-permute-start.12 = (bf16[288,384]{1,0:T(8,128)(2,1)S(1)}, bf16[288,384]{1,0:T(8,128)(2,1)}, u32[]{:S(2)}, u32[]{:S(2)}) collective-permute-start(bf16[288,384]{1,0:T(8,128)(2,1)S(1)} %get-tuple-element.14.refs_0_), channel_id=1, source_target_pairs={{0,4},{4,8},{8,12},{12,14},{14,10},{10,6},{6,2},{2,0},{1,5},{5,9},... | collective-permute-start | bytes 663560 | tf_op jit(solution)/shard_map/ppermute | solution.py:253
  22.3 1.6 %collective-permute-start.20 = (bf16[288,384]{1,0:T(8,128)(2,1)S(1)}, bf16[288,384]{1,0:T(8,128)(2,1)}, u32[]{:S(2)}, u32[]{:S(2)}) collective-permute-start(bf16[288,384]{1,0:T(8,128)(2,1)S(1)} %get-tuple-element.15.refs_0_), channel_id=1, source_target_pairs={{0,4},{4,8},{8,12},{12,14},{14,10},{10,6},{6,2},{2,0},{1,5},{5,9},... | collective-permute-start | bytes 663560 | tf_op jit(solution)/shard_map/ppermute | solution.py:253
  25.1 8.0 %collective-permute-done.9.refs_8_ = bf16[384,1536]{1,0:T(8,128)(2,1)S(1)} collective-permute-done((bf16[384,1536]{1,0:T(8,128)(2,1)S(1)}, bf16[384,1536]{1,0:T(8,128)(2,1)S(1)}, u32[]{:S(2)}, u32[]{:S(2)}) %collective-permute-start.9) | collective-permute-done | bytes 1179680 | tf_op jit(solution)/shard_map/ppermute | solution.py:232
  33.1 1.8 %collective-permute-start.2 = (bf16[288,384]{1,0:T(8,128)(2,1)S(1)}, bf16[288,384]{1,0:T(8,128)(2,1)S(1)}, u32[]{:S(2)}, u32[]{:S(2)}) collective-permute-start(bf16[288,384]{1,0:T(8,128)(2,1)S(1)} %collective-permute-done.refs_1_), channel_id=1, source_target_pairs={{0,4},{4,8},{8,12},{12,14},{14,10},{10,6},{6,2},{2,0},{1,5},{5,9},... | collective-permute-start | bytes 663560 | tf_op jit(solution)/shard_map/ppermute | solution.py:253
  35.6 1.6 %collective-permute-start.30 = (bf16[264,384]{1,0:T(8,128)(2,1)S(1)}, bf16[264,384]{1,0:T(8,128)(2,1)S(1)}, u32[]{:S(2)}, u32[]{:S(2)}) collective-permute-start(bf16[264,384]{1,0:T(8,128)(2,1)S(1)} %collective-permute-done.28.refs_1_), channel_id=1, source_target_pairs={{0,4},{4,8},{8,12},{12,14},{14,10},{10,6},{6,2},{2,0},{1,5},{5,9},... | collective-permute-start | bytes 608264 | tf_op jit(solution)/shard_map/ppermute | solution.py:253
  39.9 5.4 %collective-permute-done.30.refs_3_ = bf16[264,384]{1,0:T(8,128)(2,1)S(1)} collective-permute-done((bf16[264,384]{1,0:T(8,128)(2,1)S(1)}, bf16[264,384]{1,0:T(8,128)(2,1)S(1)}, u32[]{:S(2)}, u32[]{:S(2)}) %collective-permute-start.30) | collective-permute-done | bytes 202784 | tf_op jit(solution)/shard_map/ppermute | solution.py:253
  45.3 1.8 %collective-permute-start.14 = (bf16[288,384]{1,0:T(8,128)(2,1)}, bf16[288,384]{1,0:T(8,128)(2,1)}, u32[]{:S(2)}, u32[]{:S(2)}) collective-permute-start(bf16[288,384]{1,0:T(8,128)(2,1)} %collective-permute-done.12.refs_1_), channel_id=1, source_target_pairs={{0,4},{4,8},{8,12},{12,14},{14,10},{10,6},{6,2},{2,0},{1,5},{5,9},... | collective-permute-start | bytes 663560 | tf_op jit(solution)/shard_map/ppermute | solution.py:253
  47.3 1.8 %collective-permute-start.22 = (bf16[288,384]{1,0:T(8,128)(2,1)}, bf16[288,384]{1,0:T(8,128)(2,1)}, u32[]{:S(2)}, u32[]{:S(2)}) collective-permute-start(bf16[288,384]{1,0:T(8,128)(2,1)} %collective-permute-done.20.refs_1_), channel_id=1, source_target_pairs={{0,4},{4,8},{8,12},{12,14},{14,10},{10,6},{6,2},{2,0},{1,5},{5,9},... | collective-permute-start | bytes 663560 | tf_op jit(solution)/shard_map/ppermute | solution.py:253
  50.6 3.3 %collective-permute-done.14.refs_3_ = bf16[288,384]{1,0:T(8,128)(2,1)} collective-permute-done((bf16[288,384]{1,0:T(8,128)(2,1)}, bf16[288,384]{1,0:T(8,128)(2,1)}, u32[]{:S(2)}, u32[]{:S(2)}) %collective-permute-start.14) | collective-permute-done | bytes 221216 | tf_op jit(solution)/shard_map/ppermute | solution.py:253
  53.9 1.7 %collective-permute-start.23 = (bf16[288,384]{1,0:T(8,128)(2,1)}, bf16[288,384]{1,0:T(8,128)(2,1)S(1)}, u32[]{:S(2)}, u32[]{:S(2)}) collective-permute-start(bf16[288,384]{1,0:T(8,128)(2,1)} %copy-done.11), channel_id=1, source_target_pairs={{4,0},{8,4},{12,8},{14,12},{10,14},{6,10},{2,6},{0,2},{5,1},{9,5},... | collective-permute-start | bytes 663560 | tf_op jit(solution)/shard_map/ppermute | solution.py:255
  55.6 1.6 %collective-permute-start.33 = (bf16[264,384]{1,0:T(8,128)(2,1)}, bf16[264,384]{1,0:T(8,128)(2,1)S(1)}, u32[]{:S(2)}, u32[]{:S(2)}) collective-permute-start(bf16[264,384]{1,0:T(8,128)(2,1)} %copy-done.25), channel_id=1, source_target_pairs={{4,0},{8,4},{12,8},{14,12},{10,14},{6,10},{2,6},{0,2},{5,1},{9,5},... | collective-permute-start | bytes 608264 | tf_op jit(solution)/shard_map/ppermute | solution.py:255
  57.4 1.8 %collective-permute-start.4 = (bf16[288,384]{1,0:T(8,128)(2,1)}, bf16[288,384]{1,0:T(8,128)(2,1)S(1)}, u32[]{:S(2)}, u32[]{:S(2)}) collective-permute-start(bf16[288,384]{1,0:T(8,128)(2,1)} %copy-done.13), channel_id=1, source_target_pairs={{0,4},{4,8},{8,12},{12,14},{14,10},{10,6},{6,2},{2,0},{1,5},{5,9},... | collective-permute-start | bytes 663560 | tf_op jit(solution)/shard_map/ppermute | solution.py:253
  59.3 1.4 constant_dynamic-update-slice_fusion.1
  61.2 2.3 %collective-permute-start.5 = (bf16[288,384]{1,0:T(8,128)(2,1)S(1)}, bf16[288,384]{1,0:T(8,128)(2,1)S(1)}, u32[]{:S(2)}, u32[]{:S(2)}) collective-permute-start(bf16[288,384]{1,0:T(8,128)(2,1)S(1)} %copy-done.16), channel_id=1, source_target_pairs={{4,0},{8,4},{12,8},{14,12},{10,14},{6,10},{2,6},{0,2},{5,1},{9,5},... | collective-permute-start | bytes 663560 | tf_op jit(solution)/shard_map/ppermute | solution.py:255
  63.5 2.0 %collective-permute-done.33.refs_6_ = bf16[264,384]{1,0:T(8,128)(2,1)S(1)} collective-permute-done((bf16[264,384]{1,0:T(8,128)(2,1)}, bf16[264,384]{1,0:T(8,128)(2,1)S(1)}, u32[]{:S(2)}, u32[]{:S(2)}) %collective-permute-start.33) | collective-permute-done | bytes 202784 | tf_op jit(solution)/shard_map/ppermute | solution.py:255
  65.4 1.2 collective-permute-start.16
  66.6 1.2 collective-permute-start.17
  67.8 1.8 %collective-permute-done.5.refs_6_ = bf16[288,384]{1,0:T(8,128)(2,1)S(1)} collective-permute-done((bf16[288,384]{1,0:T(8,128)(2,1)S(1)}, bf16[288,384]{1,0:T(8,128)(2,1)S(1)}, u32[]{:S(2)}, u32[]{:S(2)}) %collective-permute-start.5) | collective-permute-done | bytes 221216 | tf_op jit(solution)/shard_map/ppermute | solution.py:255
  69.6 1.7 %collective-permute-start.24 = (bf16[288,384]{1,0:T(8,128)(2,1)}, bf16[288,384]{1,0:T(8,128)(2,1)S(1)}, u32[]{:S(2)}, u32[]{:S(2)}) collective-permute-start(bf16[288,384]{1,0:T(8,128)(2,1)} %collective-permute-done.22.refs_3_), channel_id=1, source_target_pairs={{0,4},{4,8},{8,12},{12,14},{14,10},{10,6},{6,2},{2,0},{1,5},{5,9},... | collective-permute-start | bytes 663560 | tf_op jit(solution)/shard_map/ppermute | solution.py:253
  71.4 2.9 %collective-permute-done.16.refs_5_ = bf16[288,384]{1,0:T(8,128)(2,1)S(1)} collective-permute-done((bf16[288,384]{1,0:T(8,128)(2,1)}, bf16[288,384]{1,0:T(8,128)(2,1)S(1)}, u32[]{:S(2)}, u32[]{:S(2)}) %collective-permute-start.16) | collective-permute-done | bytes 221216 | tf_op jit(solution)/shard_map/ppermute | solution.py:253
  74.4 1.9 %collective-permute-start.18 = (bf16[288,384]{1,0:T(8,128)(2,1)S(1)}, bf16[288,384]{1,0:T(8,128)(2,1)S(1)}, u32[]{:S(2)}, u32[]{:S(2)}) collective-permute-start(bf16[288,384]{1,0:T(8,128)(2,1)S(1)} %collective-permute-done.17.refs_6_), channel_id=1, source_target_pairs={{4,0},{8,4},{12,8},{14,12},{10,14},{6,10},{2,6},{0,2},{5,1},{9,5},... | collective-permute-start | bytes 663560 | tf_op jit(solution)/shard_map/ppermute | solution.py:255
  76.4 2.7 %collective-permute-done.24.refs_5_ = bf16[288,384]{1,0:T(8,128)(2,1)S(1)} collective-permute-done((bf16[288,384]{1,0:T(8,128)(2,1)}, bf16[288,384]{1,0:T(8,128)(2,1)S(1)}, u32[]{:S(2)}, u32[]{:S(2)}) %collective-permute-start.24) | collective-permute-done | bytes 221216 | tf_op jit(solution)/shard_map/ppermute | solution.py:253
  79.0 0.9 collective-permute-start.32
  80.0 1.5 collective-permute-done.6.refs_7_
  82.3 1.5 collective-permute-start.34
  84.3 1.3 constant_dynamic-update-slice_fusion
  85.7 3.4 %product.9 = f32[288,384]{1,0:T(8,128)S(1)} custom-call(s32[8]{0:T(128)S(1)} %and_select_fusion.2.at_ref, bf16[288,384]{1,0:T(8,128)(2,1)S(1)} %copy-done.6, bf16[288,384]{1,0:T(8,128)(2,1)S(1)} %copy-done.8, bf16[288,384]{1,0:T(8,128)(2,1)S(1)} %copy-done.10, bf16[288,384]{1,0:T(8,128)(2,1)S(1)} %copy-done.14, bf16[288,384]{1,0:T(8,128)(2,1)S(1)} %copy-done.16, ...), custom_call_target="tpu_custom_call" | custom-call | flops 679477248 | bytes 4571136 | tf_op jit(solution)/shard_map/product/pallas_call | solution.py:119
  89.1 4.2 %product.11 = f32[288,384]{1,0:T(8,128)S(1)} custom-call(s32[8]{0:T(128)S(1)} %and_select_fusion.at_ref, bf16[288,384]{1,0:T(8,128)(2,1)S(1)} %copy-done.4, bf16[288,384]{1,0:T(8,128)(2,1)} %collective-permute-done.12.refs_1_, bf16[288,384]{1,0:T(8,128)(2,1)} %collective-permute-done.13.refs_2_, bf16[288,384]{1,0:T(8,128)(2,1)} %collective-permute-done.14.refs_3_, ...), custom_call_target="tpu_custom_call" | custom-call | flops 679477248 | bytes 4571136 | tf_op jit(solution)/shard_map/product/pallas_call | solution.py:119
  93.4 1.4 collective-permute-start.11
  95.5 3.9 %product.13 = f32[288,384]{1,0:T(8,128)S(1)} custom-call(s32[8]{0:T(128)S(1)} %and_select_fusion.2.at_ref, bf16[288,384]{1,0:T(8,128)(2,1)S(1)} %copy-done.2, bf16[288,384]{1,0:T(8,128)(2,1)} %collective-permute-done.20.refs_1_, bf16[288,384]{1,0:T(8,128)(2,1)S(1)} %copy-done.12, bf16[288,384]{1,0:T(8,128)(2,1)} %collective-permute-done.22.refs_3_, ...), custom_call_target="tpu_custom_call" | custom-call | flops 679477248 | bytes 4571136 | tf_op jit(solution)/shard_map/product/pallas_call | solution.py:119
  99.4 1.4 collective-permute-start.27
  100.8 3.0 %product.15 = f32[264,384]{1,0:T(8,128)S(1)} custom-call(s32[8]{0:T(128)S(1)} %and_select_fusion.at_ref, bf16[264,384]{1,0:T(8,128)(2,1)S(1)} %copy-done.18, bf16[264,384]{1,0:T(8,128)(2,1)S(1)} %copy-done.20, bf16[264,384]{1,0:T(8,128)(2,1)S(1)} %copy-done.22, bf16[264,384]{1,0:T(8,128)(2,1)S(1)} %copy-done.24, bf16[264,384]{1,0:T(8,128)(2,1)S(1)} %copy-done.26, ...), custom_call_target="tpu_custom_call" | custom-call | flops 622854144 | bytes 4386816 | tf_op jit(solution)/shard_map/product/pallas_call | solution.py:119
  104.6 4.0 %fusion.refs_10_ = f32[1128,384]{1,0:T(8,128)S(1)} fusion(bf16[2256,384]{1,0:T(8,128)(2,1)S(1)} %constant_dynamic-update-slice_fusion, bf16[1128,2256]{1,0:T(8,128)(2,1)S(1)} %bitcast.10, bf16[1128,384]{1,0:T(8,128)(2,1)} %a_ref.1, f32[1128]{0:T(1024)S(1)} %select_reduce_fusion), kind=kOutput, calls=%fused_computation.1 | convolution fusion | flops 1955681280 | bytes 9425568 | tf_op jit(solution)/shard_map/dot_general | solution.py:245
  108.7 3.4 %product.8 = f32[288,384]{1,0:T(8,128)S(1)} custom-call(s32[8]{0:T(128)S(1)} %and_select_fusion.2.at_ref, bf16[288,384]{1,0:T(8,128)(2,1)S(1)} %copy-done.6, bf16[288,384]{1,0:T(8,128)(2,1)S(1)} %copy-done.8, bf16[288,384]{1,0:T(8,128)(2,1)S(1)} %copy-done.10, bf16[288,384]{1,0:T(8,128)(2,1)S(1)} %copy-done.14, bf16[288,384]{1,0:T(8,128)(2,1)S(1)} %copy-done.16, ...), custom_call_target="tpu_custom_call" | custom-call | flops 679477248 | bytes 4571136 | tf_op jit(solution)/shard_map/product/pallas_call | solution.py:119
  112.1 4.1 %product.10 = f32[288,384]{1,0:T(8,128)S(1)} custom-call(s32[8]{0:T(128)S(1)} %and_select_fusion.at_ref, bf16[288,384]{1,0:T(8,128)(2,1)S(1)} %copy-done.4, bf16[288,384]{1,0:T(8,128)(2,1)} %collective-permute-done.12.refs_1_, bf16[288,384]{1,0:T(8,128)(2,1)} %collective-permute-done.13.refs_2_, bf16[288,384]{1,0:T(8,128)(2,1)} %collective-permute-done.14.refs_3_, ...), custom_call_target="tpu_custom_call" | custom-call | flops 679477248 | bytes 4571136 | tf_op jit(solution)/shard_map/product/pallas_call | solution.py:119
  116.2 3.9 %product.12 = f32[288,384]{1,0:T(8,128)S(1)} custom-call(s32[8]{0:T(128)S(1)} %and_select_fusion.2.at_ref, bf16[288,384]{1,0:T(8,128)(2,1)S(1)} %copy-done.2, bf16[288,384]{1,0:T(8,128)(2,1)} %collective-permute-done.20.refs_1_, bf16[288,384]{1,0:T(8,128)(2,1)S(1)} %copy-done.12, bf16[288,384]{1,0:T(8,128)(2,1)} %collective-permute-done.22.refs_3_, ...), custom_call_target="tpu_custom_call" | custom-call | flops 679477248 | bytes 4571136 | tf_op jit(solution)/shard_map/product/pallas_call | solution.py:119
  120.8 4.6 %collective-permute-done.27 = f32[288,384]{1,0:T(8,128)S(1)} collective-permute-done((f32[288,384]{1,0:T(8,128)S(1)}, f32[288,384]{1,0:T(8,128)S(1)}, u32[]{:S(2)}, u32[]{:S(2)}) %collective-permute-start.27) | collective-permute-done | bytes 442400 | tf_op jit(solution)/shard_map/ppermute | solution.py:260
  125.6 2.9 %product.14 = f32[264,384]{1,0:T(8,128)S(1)} custom-call(s32[8]{0:T(128)S(1)} %and_select_fusion.at_ref, bf16[264,384]{1,0:T(8,128)(2,1)S(1)} %copy-done.18, bf16[264,384]{1,0:T(8,128)(2,1)S(1)} %copy-done.20, bf16[264,384]{1,0:T(8,128)(2,1)S(1)} %copy-done.22, bf16[264,384]{1,0:T(8,128)(2,1)S(1)} %copy-done.24, bf16[264,384]{1,0:T(8,128)(2,1)S(1)} %copy-done.26, ...), custom_call_target="tpu_custom_call" | custom-call | flops 622854144 | bytes 4386816 | tf_op jit(solution)/shard_map/product/pallas_call | solution.py:119
  128.5 2.9 %collective-permute-done.35 = f32[264,384]{1,0:T(8,128)S(1)} collective-permute-done((f32[264,384]{1,0:T(8,128)S(1)}, f32[264,384]{1,0:T(8,128)S(1)}, u32[]{:S(2)}, u32[]{:S(2)}) %collective-permute-start.35) | collective-permute-done | bytes 405536 | tf_op jit(solution)/shard_map/ppermute | solution.py:260
  131.6 1.7 %collective-permute-done.39.refs_7_ = f32[264,384]{1,0:T(8,128)S(1)} collective-permute-done((f32[264,384]{1,0:T(8,128)S(1)}, f32[264,384]{1,0:T(8,128)S(1)}, u32[]{:S(2)}, u32[]{:S(2)}) %collective-permute-start.39) | collective-permute-done | bytes 405536 | tf_op jit(solution)/shard_map/ppermute | solution.py:29
  133.3 15.9 %mirror.1 = f32[1128,384]{1,0:T(8,128)} custom-call(s32[1128]{0:T(1024)S(1)} %add_select_fusion.index_ref, f32[288,384]{1,0:T(8,128)S(1)} %add.83.refs_0_, f32[288,384]{1,0:T(8,128)S(1)} %add.86.refs_1_, f32[288,384]{1,0:T(8,128)S(1)} %add.89.refs_2_, f32[264,384]{1,0:T(8,128)S(1)} %add.92.refs_3_, f32[288,384]{1,0:T(8,128)S(1)} %collective-permute-done.36.refs_4_, ...), custom_call_target="tpu_custom_call" | custom-call | flops 433152 | bytes 5197824 | tf_op jit(solution)/shard_map/mirror/pallas_call | solution.py:178
  (127 shorter events, 15.3 us)
Async XLA Ops:
  0.0 50.4 %copy-start.30 = (f32[48]{0:T(128)S(1)}, f32[48]{0:T(128)}, u32[]{:S(2)}) copy-start(f32[48]{0:T(128)} %param.15) | copy-start | bytes 580
  0.0 50.4 %copy-start.28 = (s32[1128,2]{0,1:T(2,128)S(1)}, s32[1128,2]{0,1:T(2,128)}, u32[]{:S(2)}) copy-start(s32[1128,2]{0,1:T(2,128)} %param.16) | copy-start | bytes 27076
  4.1 29.0 %collective-permute-start.9 = (bf16[384,1536]{1,0:T(8,128)(2,1)S(1)}, bf16[384,1536]{1,0:T(8,128)(2,1)S(1)}, u32[]{:S(2)}, u32[]{:S(2)}) collective-permute-start(bf16[384,1536]{1,0:T(8,128)(2,1)S(1)} %get-tuple-element.13), channel_id=1, source_target_pairs={{0,1},{1,0},{2,3},{3,2},{4,5},{5,4},{6,7},{7,6},{8,9},{9,8},{10,11... | collective-permute-start | bytes 3538952 | tf_op jit(solution)/shard_map/ppermute | solution.py:232
  8.3 14.0 %collective-permute-start = (bf16[288,384]{1,0:T(8,128)(2,1)S(1)}, bf16[288,384]{1,0:T(8,128)(2,1)S(1)}, u32[]{:S(2)}, u32[]{:S(2)}) collective-permute-start(bf16[288,384]{1,0:T(8,128)(2,1)S(1)} %get-tuple-element.11.refs_0_), channel_id=1, source_target_pairs={{0,4},{4,8},{8,12},{12,14},{14,10},{10,6},{6,2},{2,0},{1,5},{5,9},... | collective-permute-start | bytes 663560 | tf_op jit(solution)/shard_map/ppermute | solution.py:253
  10.0 9.7 %collective-permute-start.28 = (bf16[264,384]{1,0:T(8,128)(2,1)S(1)}, bf16[264,384]{1,0:T(8,128)(2,1)S(1)}, u32[]{:S(2)}, u32[]{:S(2)}) collective-permute-start(bf16[264,384]{1,0:T(8,128)(2,1)S(1)} %get-tuple-element.16.refs_0_), channel_id=1, source_target_pairs={{0,4},{4,8},{8,12},{12,14},{14,10},{10,6},{6,2},{2,0},{1,5},{5,9},... | collective-permute-start | bytes 608264 | tf_op jit(solution)/shard_map/ppermute | solution.py:253
  11.5 9.7 %collective-permute-start.29 = (bf16[264,384]{1,0:T(8,128)(2,1)S(1)}, bf16[264,384]{1,0:T(8,128)(2,1)S(1)}, u32[]{:S(2)}, u32[]{:S(2)}) collective-permute-start(bf16[264,384]{1,0:T(8,128)(2,1)S(1)} %get-tuple-element.16.refs_0_), channel_id=1, source_target_pairs={{4,0},{8,4},{12,8},{14,12},{10,14},{6,10},{2,6},{0,2},{5,1},{9,5},... | collective-permute-start | bytes 608264 | tf_op jit(solution)/shard_map/ppermute | solution.py:255
  12.7 11.3 %collective-permute-start.1 = (bf16[288,384]{1,0:T(8,128)(2,1)S(1)}, bf16[288,384]{1,0:T(8,128)(2,1)S(1)}, u32[]{:S(2)}, u32[]{:S(2)}) collective-permute-start(bf16[288,384]{1,0:T(8,128)(2,1)S(1)} %get-tuple-element.11.refs_0_), channel_id=1, source_target_pairs={{4,0},{8,4},{12,8},{14,12},{10,14},{6,10},{2,6},{0,2},{5,1},{9,5},... | collective-permute-start | bytes 663560 | tf_op jit(solution)/shard_map/ppermute | solution.py:255
  19.6 13.4 %collective-permute-start.12 = (bf16[288,384]{1,0:T(8,128)(2,1)S(1)}, bf16[288,384]{1,0:T(8,128)(2,1)}, u32[]{:S(2)}, u32[]{:S(2)}) collective-permute-start(bf16[288,384]{1,0:T(8,128)(2,1)S(1)} %get-tuple-element.14.refs_0_), channel_id=1, source_target_pairs={{0,4},{4,8},{8,12},{12,14},{14,10},{10,6},{6,2},{2,0},{1,5},{5,9},... | collective-permute-start | bytes 663560 | tf_op jit(solution)/shard_map/ppermute | solution.py:253
  21.2 14.4 %collective-permute-start.13 = (bf16[288,384]{1,0:T(8,128)(2,1)S(1)}, bf16[288,384]{1,0:T(8,128)(2,1)}, u32[]{:S(2)}, u32[]{:S(2)}) collective-permute-start(bf16[288,384]{1,0:T(8,128)(2,1)S(1)} %get-tuple-element.14.refs_0_), channel_id=1, source_target_pairs={{4,0},{8,4},{12,8},{14,12},{10,14},{6,10},{2,6},{0,2},{5,1},{9,5},... | collective-permute-start | bytes 663560 | tf_op jit(solution)/shard_map/ppermute | solution.py:255
  22.3 15.5 %collective-permute-start.20 = (bf16[288,384]{1,0:T(8,128)(2,1)S(1)}, bf16[288,384]{1,0:T(8,128)(2,1)}, u32[]{:S(2)}, u32[]{:S(2)}) collective-permute-start(bf16[288,384]{1,0:T(8,128)(2,1)S(1)} %get-tuple-element.15.refs_0_), channel_id=1, source_target_pairs={{0,4},{4,8},{8,12},{12,14},{14,10},{10,6},{6,2},{2,0},{1,5},{5,9},... | collective-permute-start | bytes 663560 | tf_op jit(solution)/shard_map/ppermute | solution.py:253
  23.9 15.1 %collective-permute-start.21 = (bf16[288,384]{1,0:T(8,128)(2,1)S(1)}, bf16[288,384]{1,0:T(8,128)(2,1)S(1)}, u32[]{:S(2)}, u32[]{:S(2)}) collective-permute-start(bf16[288,384]{1,0:T(8,128)(2,1)S(1)} %get-tuple-element.15.refs_0_), channel_id=1, source_target_pairs={{4,0},{8,4},{12,8},{14,12},{10,14},{6,10},{2,6},{0,2},{5,1},{9,5},... | collective-permute-start | bytes 663560 | tf_op jit(solution)/shard_map/ppermute | solution.py:255
  33.1 50.7 %collective-permute-start.10 = (bf16[384,1536]{1,0:T(8,128)(2,1)S(1)}, bf16[384,1536]{1,0:T(8,128)(2,1)S(1)}, u32[]{:S(2)}, u32[]{:S(2)}) collective-permute-start(bf16[384,1536]{1,0:T(8,128)(2,1)S(1)} %collective-permute-done.9.refs_8_), channel_id=1, source_target_pairs={{0,16},{16,0},{1,17},{17,1},{2,18},{18,2},{3,19},{19,3},{4,20},{20... | collective-permute-start | bytes 3538952 | tf_op jit(solution)/shard_map/ppermute | solution.py:29
  33.1 14.2 %collective-permute-start.2 = (bf16[288,384]{1,0:T(8,128)(2,1)S(1)}, bf16[288,384]{1,0:T(8,128)(2,1)S(1)}, u32[]{:S(2)}, u32[]{:S(2)}) collective-permute-start(bf16[288,384]{1,0:T(8,128)(2,1)S(1)} %collective-permute-done.refs_1_), channel_id=1, source_target_pairs={{0,4},{4,8},{8,12},{12,14},{14,10},{10,6},{6,2},{2,0},{1,5},{5,9},... | collective-permute-start | bytes 663560 | tf_op jit(solution)/shard_map/ppermute | solution.py:253
  35.6 9.7 %collective-permute-start.30 = (bf16[264,384]{1,0:T(8,128)(2,1)S(1)}, bf16[264,384]{1,0:T(8,128)(2,1)S(1)}, u32[]{:S(2)}, u32[]{:S(2)}) collective-permute-start(bf16[264,384]{1,0:T(8,128)(2,1)S(1)} %collective-permute-done.28.refs_1_), channel_id=1, source_target_pairs={{0,4},{4,8},{8,12},{12,14},{14,10},{10,6},{6,2},{2,0},{1,5},{5,9},... | collective-permute-start | bytes 608264 | tf_op jit(solution)/shard_map/ppermute | solution.py:253
  37.8 9.2 %collective-permute-start.31 = (bf16[264,384]{1,0:T(8,128)(2,1)S(1)}, bf16[264,384]{1,0:T(8,128)(2,1)S(1)}, u32[]{:S(2)}, u32[]{:S(2)}) collective-permute-start(bf16[264,384]{1,0:T(8,128)(2,1)S(1)} %collective-permute-done.29.refs_2_), channel_id=1, source_target_pairs={{4,0},{8,4},{12,8},{14,12},{10,14},{6,10},{2,6},{0,2},{5,1},{9,5},... | collective-permute-start | bytes 608264 | tf_op jit(solution)/shard_map/ppermute | solution.py:255
  39.0 10.7 %collective-permute-start.3 = (bf16[288,384]{1,0:T(8,128)(2,1)S(1)}, bf16[288,384]{1,0:T(8,128)(2,1)S(1)}, u32[]{:S(2)}, u32[]{:S(2)}) collective-permute-start(bf16[288,384]{1,0:T(8,128)(2,1)S(1)} %collective-permute-done.1.refs_2_), channel_id=1, source_target_pairs={{4,0},{8,4},{12,8},{14,12},{10,14},{6,10},{2,6},{0,2},{5,1},{9,5},... | collective-permute-start | bytes 663560 | tf_op jit(solution)/shard_map/ppermute | solution.py:255
  45.3 8.6 %collective-permute-start.14 = (bf16[288,384]{1,0:T(8,128)(2,1)}, bf16[288,384]{1,0:T(8,128)(2,1)}, u32[]{:S(2)}, u32[]{:S(2)}) collective-permute-start(bf16[288,384]{1,0:T(8,128)(2,1)} %collective-permute-done.12.refs_1_), channel_id=1, source_target_pairs={{0,4},{4,8},{8,12},{12,14},{14,10},{10,6},{6,2},{2,0},{1,5},{5,9},... | collective-permute-start | bytes 663560 | tf_op jit(solution)/shard_map/ppermute | solution.py:253
  47.1 8.6 %collective-permute-start.15 = (bf16[288,384]{1,0:T(8,128)(2,1)}, bf16[288,384]{1,0:T(8,128)(2,1)}, u32[]{:S(2)}, u32[]{:S(2)}) collective-permute-start(bf16[288,384]{1,0:T(8,128)(2,1)} %collective-permute-done.13.refs_2_), channel_id=1, source_target_pairs={{4,0},{8,4},{12,8},{14,12},{10,14},{6,10},{2,6},{0,2},{5,1},{9,5},... | collective-permute-start | bytes 663560 | tf_op jit(solution)/shard_map/ppermute | solution.py:255
  47.3 10.0 %collective-permute-start.22 = (bf16[288,384]{1,0:T(8,128)(2,1)}, bf16[288,384]{1,0:T(8,128)(2,1)}, u32[]{:S(2)}, u32[]{:S(2)}) collective-permute-start(bf16[288,384]{1,0:T(8,128)(2,1)} %collective-permute-done.20.refs_1_), channel_id=1, source_target_pairs={{0,4},{4,8},{8,12},{12,14},{14,10},{10,6},{6,2},{2,0},{1,5},{5,9},... | collective-permute-start | bytes 663560 | tf_op jit(solution)/shard_map/ppermute | solution.py:253
  50.4 28.6 %collective-permute-start.8 = (bf16[1128,384]{1,0:T(8,128)(2,1)}, bf16[1128,384]{1,0:T(8,128)(2,1)}, u32[]{:S(2)}, u32[]{:S(2)}) collective-permute-start(bf16[1128,384]{1,0:T(8,128)(2,1)} %a_ref.1), channel_id=1, source_target_pairs={{0,16},{16,0},{1,17},{17,1},{2,18},{18,2},{3,19},{19,3},{4,20},{20... | collective-permute-start | bytes 2598920 | tf_op jit(solution)/shard_map/ppermute | solution.py:29
  50.6 25.8 %copy-start.31 = (s32[8]{0:T(128)S(1)}, s32[8]{0:T(128)}, u32[]{:S(2)}) copy-start(s32[8]{0:T(128)} %constant.141) | copy-start | bytes 100
  50.6 28.4 %copy-start.24 = (bf16[264,384]{1,0:T(8,128)(2,1)S(1)}, bf16[264,384]{1,0:T(8,128)(2,1)}, u32[]{:S(2)}) copy-start(bf16[264,384]{1,0:T(8,128)(2,1)} %copy-done.23) | copy-start | bytes 608260
  53.9 7.2 %collective-permute-start.23 = (bf16[288,384]{1,0:T(8,128)(2,1)}, bf16[288,384]{1,0:T(8,128)(2,1)S(1)}, u32[]{:S(2)}, u32[]{:S(2)}) collective-permute-start(bf16[288,384]{1,0:T(8,128)(2,1)} %copy-done.11), channel_id=1, source_target_pairs={{4,0},{8,4},{12,8},{14,12},{10,14},{6,10},{2,6},{0,2},{5,1},{9,5},... | collective-permute-start | bytes 663560 | tf_op jit(solution)/shard_map/ppermute | solution.py:255
  55.6 9.8 %collective-permute-start.33 = (bf16[264,384]{1,0:T(8,128)(2,1)}, bf16[264,384]{1,0:T(8,128)(2,1)S(1)}, u32[]{:S(2)}, u32[]{:S(2)}) collective-permute-start(bf16[264,384]{1,0:T(8,128)(2,1)} %copy-done.25), channel_id=1, source_target_pairs={{4,0},{8,4},{12,8},{14,12},{10,14},{6,10},{2,6},{0,2},{5,1},{9,5},... | collective-permute-start | bytes 608264 | tf_op jit(solution)/shard_map/ppermute | solution.py:255
  57.4 9.3 %collective-permute-start.4 = (bf16[288,384]{1,0:T(8,128)(2,1)}, bf16[288,384]{1,0:T(8,128)(2,1)S(1)}, u32[]{:S(2)}, u32[]{:S(2)}) collective-permute-start(bf16[288,384]{1,0:T(8,128)(2,1)} %copy-done.13), channel_id=1, source_target_pairs={{0,4},{4,8},{8,12},{12,14},{14,10},{10,6},{6,2},{2,0},{1,5},{5,9},... | collective-permute-start | bytes 663560 | tf_op jit(solution)/shard_map/ppermute | solution.py:253
  59.3 26.4 %copy-start.6 = (bf16[288,384]{1,0:T(8,128)(2,1)S(1)}, bf16[288,384]{1,0:T(8,128)(2,1)}, u32[]{:S(2)}) copy-start(bf16[288,384]{1,0:T(8,128)(2,1)} %copy-done.5) | copy-start | bytes 663556
  59.3 26.4 %copy-start.8 = (bf16[288,384]{1,0:T(8,128)(2,1)S(1)}, bf16[288,384]{1,0:T(8,128)(2,1)}, u32[]{:S(2)}) copy-start(bf16[288,384]{1,0:T(8,128)(2,1)} %copy-done.7) | copy-start | bytes 663556
  59.3 26.4 %copy-start.10 = (bf16[288,384]{1,0:T(8,128)(2,1)S(1)}, bf16[288,384]{1,0:T(8,128)(2,1)}, u32[]{:S(2)}) copy-start(bf16[288,384]{1,0:T(8,128)(2,1)} %copy-done.9) | copy-start | bytes 663556
  59.3 26.4 %copy-start.14 = (bf16[288,384]{1,0:T(8,128)(2,1)S(1)}, bf16[288,384]{1,0:T(8,128)(2,1)}, u32[]{:S(2)}) copy-start(bf16[288,384]{1,0:T(8,128)(2,1)} %copy-done.13) | copy-start | bytes 663556
  61.2 8.5 %collective-permute-start.5 = (bf16[288,384]{1,0:T(8,128)(2,1)S(1)}, bf16[288,384]{1,0:T(8,128)(2,1)S(1)}, u32[]{:S(2)}, u32[]{:S(2)}) collective-permute-start(bf16[288,384]{1,0:T(8,128)(2,1)S(1)} %copy-done.16), channel_id=1, source_target_pairs={{4,0},{8,4},{12,8},{14,12},{10,14},{6,10},{2,6},{0,2},{5,1},{9,5},... | collective-permute-start | bytes 663560 | tf_op jit(solution)/shard_map/ppermute | solution.py:255
  65.4 8.9 %collective-permute-start.16 = (bf16[288,384]{1,0:T(8,128)(2,1)}, bf16[288,384]{1,0:T(8,128)(2,1)S(1)}, u32[]{:S(2)}, u32[]{:S(2)}) collective-permute-start(bf16[288,384]{1,0:T(8,128)(2,1)} %collective-permute-done.14.refs_3_), channel_id=1, source_target_pairs={{0,4},{4,8},{8,12},{12,14},{14,10},{10,6},{6,2},{2,0},{1,5},{5,9},... | collective-permute-start | bytes 663560 | tf_op jit(solution)/shard_map/ppermute | solution.py:253
  66.6 7.8 %collective-permute-start.17 = (bf16[288,384]{1,0:T(8,128)(2,1)}, bf16[288,384]{1,0:T(8,128)(2,1)S(1)}, u32[]{:S(2)}, u32[]{:S(2)}) collective-permute-start(bf16[288,384]{1,0:T(8,128)(2,1)} %collective-permute-done.15.refs_4_), channel_id=1, source_target_pairs={{4,0},{8,4},{12,8},{14,12},{10,14},{6,10},{2,6},{0,2},{5,1},{9,5},... | collective-permute-start | bytes 663560 | tf_op jit(solution)/shard_map/ppermute | solution.py:255
  69.6 9.4 %collective-permute-start.24 = (bf16[288,384]{1,0:T(8,128)(2,1)}, bf16[288,384]{1,0:T(8,128)(2,1)S(1)}, u32[]{:S(2)}, u32[]{:S(2)}) collective-permute-start(bf16[288,384]{1,0:T(8,128)(2,1)} %collective-permute-done.22.refs_3_), channel_id=1, source_target_pairs={{0,4},{4,8},{8,12},{12,14},{14,10},{10,6},{6,2},{2,0},{1,5},{5,9},... | collective-permute-start | bytes 663560 | tf_op jit(solution)/shard_map/ppermute | solution.py:253
  74.3 7.1 %collective-permute-start.6 = (bf16[288,384]{1,0:T(8,128)(2,1)S(1)}, bf16[288,384]{1,0:T(8,128)(2,1)S(1)}, u32[]{:S(2)}, u32[]{:S(2)}) collective-permute-start(bf16[288,384]{1,0:T(8,128)(2,1)S(1)} %collective-permute-done.4.refs_5_), channel_id=1, source_target_pairs={{0,4},{4,8},{8,12},{12,14},{14,10},{10,6},{6,2},{2,0},{1,5},{5,9},... | collective-permute-start | bytes 663560 | tf_op jit(solution)/shard_map/ppermute | solution.py:253
  74.4 7.9 %collective-permute-start.18 = (bf16[288,384]{1,0:T(8,128)(2,1)S(1)}, bf16[288,384]{1,0:T(8,128)(2,1)S(1)}, u32[]{:S(2)}, u32[]{:S(2)}) collective-permute-start(bf16[288,384]{1,0:T(8,128)(2,1)S(1)} %collective-permute-done.17.refs_6_), channel_id=1, source_target_pairs={{4,0},{8,4},{12,8},{14,12},{10,14},{6,10},{2,6},{0,2},{5,1},{9,5},... | collective-permute-start | bytes 663560 | tf_op jit(solution)/shard_map/ppermute | solution.py:255
  79.0 29.6 %collective-permute-start.7 = (bf16[384,1536]{1,0:T(8,128)(2,1)S(1)}, bf16[384,1536]{1,0:T(8,128)(2,1)S(1)}, u32[]{:S(2)}, u32[]{:S(2)}) collective-permute-start(bf16[384,1536]{1,0:T(8,128)(2,1)S(1)} %get-tuple-element.12.refs_8_), channel_id=1, source_target_pairs={{0,16},{16,0},{1,17},{17,1},{2,18},{18,2},{3,19},{19,3},{4,20},{20... | collective-permute-start | bytes 3538952 | tf_op jit(solution)/shard_map/ppermute | solution.py:29
  79.0 20.3 %collective-permute-start.32 = (bf16[264,384]{1,0:T(8,128)(2,1)S(1)}, bf16[264,384]{1,0:T(8,128)(2,1)S(1)}, u32[]{:S(2)}, u32[]{:S(2)}) collective-permute-start(bf16[264,384]{1,0:T(8,128)(2,1)S(1)} %copy-done.24), channel_id=1, source_target_pairs={{0,4},{4,8},{8,12},{12,14},{14,10},{10,6},{6,2},{2,0},{1,5},{5,9},... | collective-permute-start | bytes 608264 | tf_op jit(solution)/shard_map/ppermute | solution.py:253
  81.4 12.0 %collective-permute-start.25 = (bf16[288,384]{1,0:T(8,128)(2,1)S(1)}, bf16[288,384]{1,0:T(8,128)(2,1)S(1)}, u32[]{:S(2)}, u32[]{:S(2)}) collective-permute-start(bf16[288,384]{1,0:T(8,128)(2,1)S(1)} %collective-permute-done.23.refs_4_), channel_id=1, source_target_pairs={{4,0},{8,4},{12,8},{14,12},{10,14},{6,10},{2,6},{0,2},{5,1},{9,5},... | collective-permute-start | bytes 663560 | tf_op jit(solution)/shard_map/ppermute | solution.py:255
  82.3 18.5 %collective-permute-start.34 = (bf16[264,384]{1,0:T(8,128)(2,1)S(1)}, bf16[264,384]{1,0:T(8,128)(2,1)S(1)}, u32[]{:S(2)}, u32[]{:S(2)}) collective-permute-start(bf16[264,384]{1,0:T(8,128)(2,1)S(1)} %collective-permute-done.33.refs_6_), channel_id=1, source_target_pairs={{4,0},{8,4},{12,8},{14,12},{10,14},{6,10},{2,6},{0,2},{5,1},{9,5},... | collective-permute-start | bytes 608264 | tf_op jit(solution)/shard_map/ppermute | solution.py:255
  83.7 11.1 %collective-permute-start.26 = (bf16[288,384]{1,0:T(8,128)(2,1)S(1)}, bf16[288,384]{1,0:T(8,128)(2,1)S(1)}, u32[]{:S(2)}, u32[]{:S(2)}) collective-permute-start(bf16[288,384]{1,0:T(8,128)(2,1)S(1)} %collective-permute-done.24.refs_5_), channel_id=1, source_target_pairs={{0,4},{4,8},{8,12},{12,14},{14,10},{10,6},{6,2},{2,0},{1,5},{5,9},... | collective-permute-start | bytes 663560 | tf_op jit(solution)/shard_map/ppermute | solution.py:253
  93.4 26.7 %collective-permute-start.11 = (f32[288,384]{1,0:T(8,128)S(1)}, f32[288,384]{1,0:T(8,128)S(1)}, u32[]{:S(2)}, u32[]{:S(2)}) collective-permute-start(f32[288,384]{1,0:T(8,128)S(1)} %product.9), channel_id=1, source_target_pairs={{0,1},{1,0},{2,3},{3,2},{4,5},{5,4},{6,7},{7,6},{8,9},{9,8},{10,11... | collective-permute-start | bytes 1327112 | tf_op jit(solution)/shard_map/ppermute | solution.py:260
  94.8 25.4 %collective-permute-start.19 = (f32[288,384]{1,0:T(8,128)S(1)}, f32[288,384]{1,0:T(8,128)S(1)}, u32[]{:S(2)}, u32[]{:S(2)}) collective-permute-start(f32[288,384]{1,0:T(8,128)S(1)} %product.11), channel_id=1, source_target_pairs={{0,1},{1,0},{2,3},{3,2},{4,5},{5,4},{6,7},{7,6},{8,9},{9,8},{10,11... | collective-permute-start | bytes 1327112 | tf_op jit(solution)/shard_map/ppermute | solution.py:260
  99.4 26.1 %collective-permute-start.27 = (f32[288,384]{1,0:T(8,128)S(1)}, f32[288,384]{1,0:T(8,128)S(1)}, u32[]{:S(2)}, u32[]{:S(2)}) collective-permute-start(f32[288,384]{1,0:T(8,128)S(1)} %product.13), channel_id=1, source_target_pairs={{0,1},{1,0},{2,3},{3,2},{4,5},{5,4},{6,7},{7,6},{8,9},{9,8},{10,11... | collective-permute-start | bytes 1327112 | tf_op jit(solution)/shard_map/ppermute | solution.py:260
  103.9 27.5 %collective-permute-start.35 = (f32[264,384]{1,0:T(8,128)S(1)}, f32[264,384]{1,0:T(8,128)S(1)}, u32[]{:S(2)}, u32[]{:S(2)}) collective-permute-start(f32[264,384]{1,0:T(8,128)S(1)} %product.15), channel_id=1, source_target_pairs={{0,1},{1,0},{2,3},{3,2},{4,5},{5,4},{6,7},{7,6},{8,9},{9,8},{10,11... | collective-permute-start | bytes 1216520 | tf_op jit(solution)/shard_map/ppermute | solution.py:260
  120.1 13.1 %collective-permute-start.36 = (f32[288,384]{1,0:T(8,128)S(1)}, f32[288,384]{1,0:T(8,128)S(1)}, u32[]{:S(2)}, u32[]{:S(2)}) collective-permute-start(f32[288,384]{1,0:T(8,128)S(1)} %add.83.refs_0_), channel_id=1, source_target_pairs={{0,16},{16,0},{1,17},{17,1},{2,18},{18,2},{3,19},{19,3},{4,20},{20... | collective-permute-start | bytes 1327112 | tf_op jit(solution)/shard_map/ppermute | solution.py:29
  120.3 13.0 %collective-permute-start.37 = (f32[288,384]{1,0:T(8,128)S(1)}, f32[288,384]{1,0:T(8,128)S(1)}, u32[]{:S(2)}, u32[]{:S(2)}) collective-permute-start(f32[288,384]{1,0:T(8,128)S(1)} %add.86.refs_1_), channel_id=1, source_target_pairs={{0,16},{16,0},{1,17},{17,1},{2,18},{18,2},{3,19},{19,3},{4,20},{20... | collective-permute-start | bytes 1327112 | tf_op jit(solution)/shard_map/ppermute | solution.py:29
  125.5 7.7 %collective-permute-start.38 = (f32[288,384]{1,0:T(8,128)S(1)}, f32[288,384]{1,0:T(8,128)S(1)}, u32[]{:S(2)}, u32[]{:S(2)}) collective-permute-start(f32[288,384]{1,0:T(8,128)S(1)} %add.89.refs_2_), channel_id=1, source_target_pairs={{0,16},{16,0},{1,17},{17,1},{2,18},{18,2},{3,19},{19,3},{4,20},{20... | collective-permute-start | bytes 1327112 | tf_op jit(solution)/shard_map/ppermute | solution.py:29
  131.4 1.8 %collective-permute-start.39 = (f32[264,384]{1,0:T(8,128)S(1)}, f32[264,384]{1,0:T(8,128)S(1)}, u32[]{:S(2)}, u32[]{:S(2)}) collective-permute-start(f32[264,384]{1,0:T(8,128)S(1)} %add.92.refs_3_), channel_id=1, source_target_pairs={{0,16},{16,0},{1,17},{17,1},{2,18},{18,2},{3,19},{19,3},{4,20},{20... | collective-permute-start | bytes 1216520 | tf_op jit(solution)/shard_map/ppermute | solution.py:29
  (27 other events, 135.3 us)

commit v2 on v1

v2 whole, which is shorter than its diff:
```python
import functools

import jax
import jax.numpy as jnp
from jax import lax
from jax.experimental import pallas as pl
from jax.experimental.pallas import tpu as pltpu
from jax.sharding import PartitionSpec as P


TILE = 128
SHARES = (384, 312, 240, 192)


LIMIT = 16 * 1024 * 1024
MIRROR_LIMIT = 24 * 1024 * 1024

SMEM = pl.BlockSpec(memory_space=pltpu.SMEM)
VMEM = pl.BlockSpec(memory_space=pltpu.VMEM)
ANY = pl.BlockSpec(memory_space=pl.ANY)


def row_chunks(rows, shares):
    edges = [0]
    for k in range(1, len(shares)):
        edges.append(rows * sum(shares[:k]) // sum(shares) // 8 * 8)
    edges.append(rows)
    return [(a, b - a) for a, b in zip(edges, edges[1:]) if b > a]


def other_core(a):
    return lax.ppermute(a, "occ", [(0, 1), (1, 0)])


def rows_kernel(chunks, a_ref, *refs):
    for (start, length), out in zip(chunks, refs):
        out[...] = a_ref[start : start + length, :]


def split_rows(a, chunks):
    return pl.pallas_call(
        functools.partial(rows_kernel, chunks),
        out_shape=[jax.ShapeDtypeStruct((length, a.shape[1]), a.dtype) for _, length in chunks],
        in_specs=[VMEM],
        out_specs=[VMEM] * len(chunks),
        compiler_params=pltpu.CompilerParams(vmem_limit_bytes=LIMIT),
        cost_estimate=pl.CostEstimate(flops=0, bytes_accessed=2 * a.size * 2, transcendentals=0),
        name="split_rows",
    )(a)


def sides_kernel(where_ref, map_hbm, v_hbm, send_ref, kept_ref, map_ref, v_ref, sems):
    side, first_row, first_col = where_ref[0], where_ref[1], where_ref[2]
    cols = v_ref.shape[0]
    tiles = cols // TILE
    map_copy = pltpu.make_async_copy(map_hbm, map_ref, sems.at[tiles])
    map_copy.start()

    def bands(r):
        band = pl.ds(r * TILE, TILE)
        return pltpu.make_async_copy(v_hbm.at[band], v_ref.at[band], sems.at[r])

    for r in range(tiles):
        bands(r).start()
    map_copy.wait()
    for r in range(tiles):
        bands(r).wait()
        for out, which in ((send_ref, 1 - side), (kept_ref, side)):
            for j in range(out.shape[1] // cols):
                block = 2 * j + which
                for c in range(tiles):
                    allowed = map_ref[first_row + r, first_col + block * tiles + c]
                    at = pl.multiple_of(block * cols + c * TILE, TILE)
                    tile = v_ref[r * TILE : (r + 1) * TILE, pl.ds(at, TILE)]
                    to = j * cols + c * TILE
                    out[r * TILE : (r + 1) * TILE, to : to + TILE] = jnp.where(
                        allowed == 1, tile, jnp.zeros_like(tile)
                    )


def split_sides(where, tile_map, integrals):
    cols, width = integrals.shape
    half = jax.ShapeDtypeStruct((cols, width // 2), integrals.dtype)
    return pl.pallas_call(
        sides_kernel,
        out_shape=[half, half],
        in_specs=[SMEM, ANY, ANY],
        out_specs=[VMEM, VMEM],
        scratch_shapes=[
            pltpu.SMEM(tile_map.shape, tile_map.dtype),
            pltpu.VMEM(integrals.shape, integrals.dtype),
            pltpu.SemaphoreType.DMA((cols // TILE + 1,)),
        ],
        compiler_params=pltpu.CompilerParams(vmem_limit_bytes=LIMIT),
        cost_estimate=pl.CostEstimate(
            flops=integrals.size, bytes_accessed=4 * integrals.size, transcendentals=0
        ),
        name="split_sides",
    )(where, tile_map, integrals)


def prepare_kernel(at_ref, *refs):
    *pieces, out_ref = refs
    cols = out_ref.shape[1]
    per_piece = pieces[0].shape[1] // cols
    for k in range(out_ref.shape[0] // cols):
        for p, piece in enumerate(pieces):
            at = at_ref[k] - p * per_piece

            @pl.when((at >= 0) & (at < per_piece))
            def _():
                block = piece[:, pl.ds(pl.multiple_of(at * cols, cols), cols)]
                out_ref[k * cols : (k + 1) * cols, :] = block.T


def prepare(at, pieces):
    cols = pieces[0].shape[0]
    depth = sum(piece.shape[1] for piece in pieces)
    return pl.pallas_call(
        prepare_kernel,
        out_shape=jax.ShapeDtypeStruct((depth, cols), pieces[0].dtype),
        in_specs=[SMEM] + [VMEM] * len(pieces),
        out_specs=VMEM,
        compiler_params=pltpu.CompilerParams(vmem_limit_bytes=LIMIT),
        cost_estimate=pl.CostEstimate(
            flops=0, bytes_accessed=4 * depth * cols, transcendentals=0
        ),
        name="prepare",
    )(at, *pieces)


def product_kernel(count, start, *refs):
    blocks = refs[:count]
    outs = len(refs[count:]) // 2
    integrals = refs[count : count + outs]
    base = None if start is None else refs[count + outs]
    row = jnp.concatenate([block[...] for block in blocks], axis=1)
    for k, out in enumerate(refs[-outs:]):
        result = jnp.dot(row, integrals[k][...], preferred_element_type=jnp.float32)
        if base is not None and k == outs - 1:
            result = result + base[start : start + out.shape[0], :]
        out[...] = result


def product(blocks, integrals, base=None, start=None):
    count = len(blocks)
    length, cols = blocks[0].shape
    given = [] if base is None else [base]
    return pl.pallas_call(
        functools.partial(product_kernel, count, start),
        out_shape=[jax.ShapeDtypeStruct((length, cols), jnp.float32)] * len(integrals),
        in_specs=[VMEM] * (count + len(integrals) + len(given)),
        out_specs=[VMEM] * len(integrals),
        compiler_params=pltpu.CompilerParams(vmem_limit_bytes=LIMIT),
        cost_estimate=pl.CostEstimate(
            flops=2 * len(integrals) * count * length * cols * cols,
            bytes_accessed=2 * count * (length + len(integrals) * cols) * cols,
            transcendentals=0,
        ),
        name="product",
    )(*blocks, *integrals, *given)


def for_groups(count, most, body):
    inline = max(u for u in range(1, most + 1) if count % u == 0)

    def step(i, carry):
        for u in range(inline):
            body(i * inline + u)
        return carry

    lax.fori_loop(0, count // inline, step, 0)


def mirror_kernel(offsets, own_count, index_ref, *refs):
    *pieces, out_ref, whole, picked = refs
    rows, cols = out_ref.shape
    lanes = cols // TILE

    for piece, offset in zip(pieces, offsets):

        def spread(g):
            at = pl.multiple_of(g * 8, 8)
            for c in range(lanes):
                whole[pl.ds(offset + at, 8), c, :] = piece[pl.ds(at, 8), c * TILE : (c + 1) * TILE]

        for_groups(piece.shape[0] // 8, 6, spread)

    def pick(g):
        for j in range(8):
            picked[g, :, j, :] = whole[index_ref[g * 8 + j]]

    for_groups(rows // 8, 6, pick)
    for j in range(rows % 8):
        picked[rows // 8, :, j, :] = whole[index_ref[rows // 8 * 8 + j]]

    odd = lax.broadcasted_iota(jnp.int32, (8, TILE), 1) % 2 == 1

    def finish(own, offset, g, size):
        at = g * 8 if isinstance(g, int) else pl.multiple_of(g * 8, 8)
        for c in range(lanes):
            part = picked[offset // 8 + g, c]
            swapped = jnp.where(odd, pltpu.roll(part, 1, 1), pltpu.roll(part, TILE - 1, 1))
            out_ref[pl.ds(offset + at, size), c * TILE : (c + 1) * TILE] = (
                own[pl.ds(at, size), c * TILE : (c + 1) * TILE] + swapped[:size]
            )

    for own, offset in zip(pieces[:own_count], offsets):
        length = min(own.shape[0], rows - offset)
        for_groups(length // 8, 48, functools.partial(finish, own, offset, size=8))
        if length % 8:
            finish(own, offset, length // 8, length % 8)


def add_mirror(index, rows, own, others):
    cols = own[0].shape[1]
    offsets, total = [], 0
    for piece in (*own, *others):
        offsets.append(total)
        total += piece.shape[0]
    return pl.pallas_call(
        functools.partial(mirror_kernel, tuple(offsets), len(own)),
        out_shape=jax.ShapeDtypeStruct((rows, cols), jnp.float32),
        in_specs=[SMEM] + [VMEM] * (len(own) + len(others)),
        out_specs=VMEM,
        scratch_shapes=[
            pltpu.VMEM((total, cols // TILE, TILE), jnp.float32),
            pltpu.VMEM((-(-rows // 8), cols // TILE, 8, TILE), jnp.float32),
        ],
        compiler_params=pltpu.CompilerParams(vmem_limit_bytes=MIRROR_LIMIT),
        cost_estimate=pl.CostEstimate(
            flops=rows * cols, bytes_accessed=(total + rows) * cols * 4, transcendentals=0
        ),
        name="mirror",
    )(index, *own, *others)


def shards(cores, chips, amplitudes, ladder_ints, tile_map, hole_ints, occ_energy, pair_list, mirror_row):
    rows, cols = amplitudes.shape
    integral_cols = ladder_ints.shape[1]
    vir_place = lax.axis_index("vir")
    occ_place = lax.axis_index("occ")
    members = chips // 2
    half_blocks = integral_cols // cols // 2
    side = vir_place % 2
    group = vir_place // 2
    across = [(v, v ^ 1) for v in range(chips)]

    evens = (members + 1) // 2
    order = [2 * p if p < evens else 2 * (members - p) - 1 for p in range(members)]
    forward, backward = [], []
    for s in range(2):
        for k in range(members):
            here, there = 2 * order[k] + s, 2 * order[(k + 1) % members] + s
            forward.append((here, there))
            backward.append((there, here))
    place = jnp.where(group % 2 == 0, group // 2, members - (group + 1) // 2)
    own_half = occ_place * half_blocks if cores == 2 else 0

    ring_steps = sorted([*range((members + 1) // 2), *range(-(members // 2), 0)], key=abs)

    def positions():
        p = (place - jnp.array(ring_steps, jnp.int32)) % members
        g = jnp.where(p < evens, 2 * p, 2 * (members - p) - 1)
        return (g - own_half) % members

    def whole_k(a):
        if cores == 2:
            return [a, other_core(a)]
        return [lax.all_gather(a, "occ", axis=1, tiled=True)]

    chunks = row_chunks(rows, SHARES)
    mine = split_rows(amplitudes, chunks)

    where = jnp.stack([side, vir_place * (cols // TILE), occ_place * (integral_cols // TILE)])
    send, kept = split_sides(where.astype(jnp.int32), tile_map, ladder_ints)
    near = lax.ppermute(send, "vir", across)
    at = positions().astype(jnp.int32)
    kept_all = prepare(at, whole_k(kept))
    near_all = prepare(at, whole_k(near))

    if cores == 2:
        both = jnp.zeros((2 * rows, cols), amplitudes.dtype)
        both = lax.dynamic_update_slice(both, amplitudes, (occ_place * rows, 0))
        both = lax.dynamic_update_slice(both, other_core(amplitudes), ((1 - occ_place) * rows, 0))
    else:
        both = lax.all_gather(amplitudes, "occ", axis=0, tiled=True)
    orbital_ids = jnp.arange(occ_energy.shape[0], dtype=jnp.int32)
    one_hot = (pair_list[:, :, None] == orbital_ids[None, None, :]).astype(jnp.float32)
    pair_energy = jnp.sum(one_hot * occ_energy[None, None, :], axis=(1, 2))
    base = jnp.dot(hole_ints, both, preferred_element_type=jnp.float32)
    base = base - pair_energy[:, None] * amplitudes.astype(jnp.float32)

    raws = []
    for index, (start, length) in enumerate(chunks):
        ups = members // 2 if index % 2 == 0 else (members - 1) // 2
        blocks = {0: mine[index]}
        for step in range(1, ups + 1):
            blocks[step] = lax.ppermute(blocks[step - 1], "vir", forward)
        for step in range(1, members - ups):
            blocks[-step] = lax.ppermute(blocks[1 - step], "vir", backward)
        arrived = [blocks[step] if step in blocks else blocks[step + members] for step in ring_steps]
        if index < len(chunks) - 1:
            for_near, rest = product(arrived, [near_all, kept_all], base, start)
        else:
            (for_near,) = product(arrived, [near_all])
            (rest,) = product(arrived, [kept_all], base, start)
        from_near = lax.ppermute(for_near, "vir", across)
        raws.append(rest + from_near)

    if cores == 2:
        others = [other_core(raw) for raw in raws]
        return add_mirror((mirror_row - occ_place * rows) % (2 * rows), rows, raws, others)
    own = jnp.concatenate(raws, axis=0)
    whole = lax.all_gather(own, "occ", axis=0, tiled=True)
    padded = -(-rows // 8) * 8
    own = jnp.pad(own, ((0, padded - rows), (0, 0)))
    return add_mirror(mirror_row + padded, rows, [own], [whole])


def solution(mesh):
    cores, chips = mesh.shape["occ"], mesh.shape["vir"]

    def body(*arrays):
        return shards(cores, chips, *arrays)

    return jax.shard_map(
        body,
        mesh=mesh,
        in_specs=(
            P("occ", "vir"),
            P("vir", "occ"),
            P(),
            P("occ", None),
            P(),
            P("occ", None),
            P("occ"),
        ),
        out_specs=P("occ", "vir"),
        check_vma=False,
    )
```

time: 150 us -> 134 us (0.89)
  Pallas kernels: 47.5 us -> 25.8 us
  waiting for transfers between devices: 43.7 us -> 55 us
  local copies, waits for them, and re-layouts: 11.6 us -> 8.11 us
  starting transfers between devices: 41.4 us -> 39 us
    pallas_call x10 -> x9, Pallas kernels: 46.2 us -> 25 us  [the longest x5 10.7 us: product(): pl.pallas_call(functools.partial(product_kernel, count, start), out_shape...]
    ppermute x14, waiting for transfers between devices: 21.7 us -> 3.47 us  [shards(): blocks[step] = lax.ppermute(blocks[step - 1], 'vir', forward)]
    ppermute x14, waiting for transfers between devices: 4.74 us -> 22.8 us  [shards(): blocks[-step] = lax.ppermute(blocks[1 - step], 'vir', backward)]
    ppermute x1, waiting for transfers between devices: 8 us -> 13.9 us  [shards(): near = lax.ppermute(send, 'vir', across)]
    ppermute x4, waiting for transfers between devices: 7.52 us -> 13.3 us  [shards(): from_near = lax.ppermute(for_near, 'vir', across)]
    unnamed x70 -> x30, local copies, waits for them, and re-layouts: 8.7 us -> 3.62 us
    ppermute x14, starting transfers between devices: 13.7 us -> 11.6 us  [shards(): blocks[-step] = lax.ppermute(blocks[1 - step], 'vir', backward)]
  transfers between devices with their start and end apart: 40 -> 40, of which waited for: 15 -> 13; matrix products, arithmetic and copies ran while one was open for 5% -> 8% of each run, Pallas kernels for 20% -> 12%
where the time goes in v2:
time: 134 us
  waiting for transfers between devices  55 us (41%)
  starting transfers between devices  39 us (29%)
  Pallas kernels  25.8 us (19%)
  local copies, waits for them, and re-layouts  8.11 us (6%)
  matrix products  5.35 us (4%)
    ppermute x14, waiting for transfers between devices, shards(): blocks[-step] = lax.ppermute(blocks[1 - step], 'vir', backward)  22.8 us
    ppermute x14, starting transfers between devices, shards(): blocks[step] = lax.ppermute(blocks[step - 1], 'vir', forward)  19.5 us
    ppermute x1, waiting for transfers between devices, shards(): near = lax.ppermute(send, 'vir', across)  13.9 us
    ppermute x4, waiting for transfers between devices, shards(): from_near = lax.ppermute(for_near, 'vir', across)  13.3 us
    ppermute x14, starting transfers between devices, shards(): blocks[-step] = lax.ppermute(blocks[1 - step], 'vir', backward)  11.6 us
    pallas_call x5, Pallas kernels, product(): pl.pallas_call(functools.partial(product_kernel, count, start), out_shape...  10.7 us
    pallas_call x1, Pallas kernels, add_mirror(): pl.pallas_call(functools.partial(mirror_kernel, tuple(offsets), len(own))...  7.15 us
    dot_general x1, matrix products, shards(): base = jnp.dot(hole_ints, both, preferred_element_type=jnp.float32)  5.35 us
  transfers between devices with their start and end apart: 40, of which 13 were waited for; matrix products, arithmetic and copies ran while one was open for 8% of the time, Pallas kernels for 12%

profile of v2, /device:TPU:0, one launch (start us, length us, event | category | flops | bytes accessed | tf_op | source)
XLA Modules:
  0.0 134.1 jit_solution(15098959585513620806)
XLA Ops:
  0.1 1.7 %copy-done.1 = bf16[384,3072]{1,0:T(8,128)(2,1)S(1)} copy-done((bf16[384,3072]{1,0:T(8,128)(2,1)S(1)}, bf16[384,3072]{1,0:T(8,128)(2,1)}, u32[]{:S(2)}) %copy-start.1) | copy-done | bytes 2359320
  2.6 2.2 %split_sides.1 = (bf16[384,1536]{1,0:T(8,128)(2,1)S(1)}, bf16[384,1536]{1,0:T(8,128)(2,1)S(1)}) custom-call(s32[3]{0:T(128)S(1)} %pad_add_fusion.where_ref, s32[48,48]{1,0:T(8,128)S(1)} %copy-done.10, bf16[384,3072]{1,0:T(8,128)(2,1)S(1)} %copy-done.1), custom_call_target="tpu_custom_call" | custom-call | flops 1179648 | bytes 4718592 | tf_op jit(solution)/shard_map/split_sides/pallas_call | solution.py:84
  4.7 3.0 %collective-permute-start.7 = (bf16[384,1536]{1,0:T(8,128)(2,1)S(1)}, bf16[384,1536]{1,0:T(8,128)(2,1)S(1)}, u32[]{:S(2)}, u32[]{:S(2)}) collective-permute-start(bf16[384,1536]{1,0:T(8,128)(2,1)S(1)} %get-tuple-element.18), channel_id=1, source_target_pairs={{0,1},{1,0},{2,3},{3,2},{4,5},{5,4},{6,7},{7,6},{8,9},{9,8},{10,11... | collective-permute-start | bytes 3538952 | tf_op jit(solution)/shard_map/ppermute | solution.py:277
  7.8 0.9 split_rows.1
  8.6 1.6 %collective-permute-start.28 = (bf16[192,384]{1,0:T(8,128)(2,1)S(1)}, bf16[192,384]{1,0:T(8,128)(2,1)S(1)}, u32[]{:S(2)}, u32[]{:S(2)}) collective-permute-start(bf16[192,384]{1,0:T(8,128)(2,1)S(1)} %get-tuple-element.28.refs_0_), channel_id=1, source_target_pairs={{0,4},{4,8},{8,12},{12,14},{14,10},{10,6},{6,2},{2,0},{1,5},{5,9},... | collective-permute-start | bytes 442376 | tf_op jit(solution)/shard_map/ppermute | solution.py:299
  10.2 1.6 %collective-permute-start.12 = (bf16[312,384]{1,0:T(8,128)(2,1)}, bf16[312,384]{1,0:T(8,128)(2,1)}, u32[]{:S(2)}, u32[]{:S(2)}) collective-permute-start(bf16[312,384]{1,0:T(8,128)(2,1)} %get-tuple-element.22.refs_0_), channel_id=1, source_target_pairs={{0,4},{4,8},{8,12},{12,14},{14,10},{10,6},{6,2},{2,0},{1,5},{5,9},... | collective-permute-start | bytes 718856 | tf_op jit(solution)/shard_map/ppermute | solution.py:299
  11.8 1.6 %collective-permute-start.20 = (bf16[240,384]{1,0:T(8,128)(2,1)S(1)}, bf16[240,384]{1,0:T(8,128)(2,1)S(1)}, u32[]{:S(2)}, u32[]{:S(2)}) collective-permute-start(bf16[240,384]{1,0:T(8,128)(2,1)S(1)} %get-tuple-element.25.refs_0_), channel_id=1, source_target_pairs={{0,4},{4,8},{8,12},{12,14},{14,10},{10,6},{6,2},{2,0},{1,5},{5,9},... | collective-permute-start | bytes 552968 | tf_op jit(solution)/shard_map/ppermute | solution.py:299
  13.8 1.5 %collective-permute-done.28.refs_1_ = bf16[192,384]{1,0:T(8,128)(2,1)S(1)} collective-permute-done((bf16[192,384]{1,0:T(8,128)(2,1)S(1)}, bf16[192,384]{1,0:T(8,128)(2,1)S(1)}, u32[]{:S(2)}, u32[]{:S(2)}) %collective-permute-start.28) | collective-permute-done | bytes 147488 | tf_op jit(solution)/shard_map/ppermute | solution.py:299
  15.4 1.5 %collective-permute-start.21 = (bf16[240,384]{1,0:T(8,128)(2,1)S(1)}, bf16[240,384]{1,0:T(8,128)(2,1)S(1)}, u32[]{:S(2)}, u32[]{:S(2)}) collective-permute-start(bf16[240,384]{1,0:T(8,128)(2,1)S(1)} %get-tuple-element.25.refs_0_), channel_id=1, source_target_pairs={{4,0},{8,4},{12,8},{14,12},{10,14},{6,10},{2,6},{0,2},{5,1},{9,5},... | collective-permute-start | bytes 552968 | tf_op jit(solution)/shard_map/ppermute | solution.py:301
  17.6 2.3 %collective-permute-done.29.refs_2_ = bf16[192,384]{1,0:T(8,128)(2,1)S(1)} collective-permute-done((bf16[192,384]{1,0:T(8,128)(2,1)S(1)}, bf16[192,384]{1,0:T(8,128)(2,1)S(1)}, u32[]{:S(2)}, u32[]{:S(2)}) %collective-permute-start.29) | collective-permute-done | bytes 147488 | tf_op jit(solution)/shard_map/ppermute | solution.py:301
  19.8 13.9 %collective-permute-done.7.refs_0_ = bf16[384,1536]{1,0:T(8,128)(2,1)S(1)} collective-permute-done((bf16[384,1536]{1,0:T(8,128)(2,1)S(1)}, bf16[384,1536]{1,0:T(8,128)(2,1)S(1)}, u32[]{:S(2)}, u32[]{:S(2)}) %collective-permute-start.7) | collective-permute-done | bytes 1179680 | tf_op jit(solution)/shard_map/ppermute | solution.py:277
  33.7 1.9 %collective-permute-start = (bf16[384,384]{1,0:T(8,128)(2,1)}, bf16[384,384]{1,0:T(8,128)(2,1)}, u32[]{:S(2)}, u32[]{:S(2)}) collective-permute-start(bf16[384,384]{1,0:T(8,128)(2,1)} %get-tuple-element.17.refs_0_), channel_id=1, source_target_pairs={{0,4},{4,8},{8,12},{12,14},{14,10},{10,6},{6,2},{2,0},{1,5},{5,9},... | collective-permute-start | bytes 884744 | tf_op jit(solution)/shard_map/ppermute | solution.py:299
  36.9 7.7 %collective-permute-done.13.refs_2_ = bf16[312,384]{1,0:T(8,128)(2,1)} collective-permute-done((bf16[312,384]{1,0:T(8,128)(2,1)}, bf16[312,384]{1,0:T(8,128)(2,1)}, u32[]{:S(2)}, u32[]{:S(2)}) %collective-permute-start.13) | collective-permute-done | bytes 239648 | tf_op jit(solution)/shard_map/ppermute | solution.py:301
  44.5 0.9 collective-permute-start.1
  45.4 1.1 collective-permute-start.2
  46.6 1.3 %broadcast_in_dim.2 = bf16[2256,384]{1,0:T(8,128)(2,1)} broadcast(bf16[]{:T(256)} %constant.101.clone.1), dimensions={} | broadcast | bytes 1732610 | tf_op jit(solution)/shard_map/broadcast_in_dim | solution.py:283
  47.9 1.0 constant_dynamic-update-slice_fusion.1
  48.9 4.1 %collective-permute-done.1.refs_2_ = bf16[384,384]{1,0:T(8,128)(2,1)} collective-permute-done((bf16[384,384]{1,0:T(8,128)(2,1)}, bf16[384,384]{1,0:T(8,128)(2,1)}, u32[]{:S(2)}, u32[]{:S(2)}) %collective-permute-start.1) | collective-permute-done | bytes 294944 | tf_op jit(solution)/shard_map/ppermute | solution.py:301
  53.1 1.2 collective-permute-start.3
  54.3 0.8 collective-permute-start.4
  55.3 1.3 collective-permute-start.15
  56.6 2.2 %constant_dynamic-update-slice_fusion = bf16[2256,384]{1,0:T(8,128)(2,1)} fusion(bf16[2256,384]{1,0:T(8,128)(2,1)} %constant_dynamic-update-slice_fusion.1, bf16[1128,384]{1,0:T(8,128)(2,1)} %collective-permute-done.10, s32[]{:T(128)S(6)} %select_n.61), kind=kLoop, calls=%fused_computation.17 | loop fusion | bytes 1732612 | tf_op jit(solution)/shard_map/dynamic_update_slice | solution.py:285
  58.7 7.1 %collective-permute-done.15.refs_4_ = bf16[312,384]{1,0:T(8,128)(2,1)S(1)} collective-permute-done((bf16[312,384]{1,0:T(8,128)(2,1)}, bf16[312,384]{1,0:T(8,128)(2,1)S(1)}, u32[]{:S(2)}, u32[]{:S(2)}) %collective-permute-start.15) | collective-permute-done | bytes 239648 | tf_op jit(solution)/shard_map/ppermute | solution.py:301
  65.8 1.6 %collective-permute-start.22 = (bf16[240,384]{1,0:T(8,128)(2,1)S(1)}, bf16[240,384]{1,0:T(8,128)(2,1)S(1)}, u32[]{:S(2)}, u32[]{:S(2)}) collective-permute-start(bf16[240,384]{1,0:T(8,128)(2,1)S(1)} %copy-done.7), channel_id=1, source_target_pairs={{0,4},{4,8},{8,12},{12,14},{14,10},{10,6},{6,2},{2,0},{1,5},{5,9},... | collective-permute-start | bytes 552968 | tf_op jit(solution)/shard_map/ppermute | solution.py:299
  67.4 1.6 %collective-permute-start.14 = (bf16[312,384]{1,0:T(8,128)(2,1)}, bf16[312,384]{1,0:T(8,128)(2,1)S(1)}, u32[]{:S(2)}, u32[]{:S(2)}) collective-permute-start(bf16[312,384]{1,0:T(8,128)(2,1)} %collective-permute-done.12.refs_1_), channel_id=1, source_target_pairs={{0,4},{4,8},{8,12},{12,14},{14,10},{10,6},{6,2},{2,0},{1,5},{5,9},... | collective-permute-start | bytes 718856 | tf_op jit(solution)/shard_map/ppermute | solution.py:299
  69.9 1.6 %collective-permute-start.6 = (bf16[384,384]{1,0:T(8,128)(2,1)}, bf16[384,384]{1,0:T(8,128)(2,1)S(1)}, u32[]{:S(2)}, u32[]{:S(2)}) collective-permute-start(bf16[384,384]{1,0:T(8,128)(2,1)} %collective-permute-done.4.refs_5_), channel_id=1, source_target_pairs={{0,4},{4,8},{8,12},{12,14},{14,10},{10,6},{6,2},{2,0},{1,5},{5,9},... | collective-permute-start | bytes 884744 | tf_op jit(solution)/shard_map/ppermute | solution.py:299
  71.4 5.4 %fusion.refs_10_.refs_9_ = f32[1128,384]{1,0:T(8,128)S(1)} fusion(bf16[2256,384]{1,0:T(8,128)(2,1)} %constant_dynamic-update-slice_fusion, bf16[1128,2256]{1,0:T(8,128)(2,1)} %param.11, bf16[1128,384]{1,0:T(8,128)(2,1)S(1)} %copy-done, f32[1128]{0:T(1024)S(1)} %select_reduce_fusion), kind=kOutput, calls=%fused_computation.1 | convolution fusion | flops 1955681280 | bytes 9425568 | tf_op jit(solution)/shard_map/dot_general | solution.py:291
  76.8 2.5 %prepare.3.refs_9_.refs_8_ = bf16[3072,384]{1,0:T(8,128)(2,1)S(1)} custom-call(s32[8]{0:T(128)S(1)} %and_select_fusion.at_ref, bf16[384,1536]{1,0:T(8,128)(2,1)S(1)} %get-tuple-element.19.refs_0_, bf16[384,1536]{1,0:T(8,128)(2,1)} %collective-permute-done.9.refs_1_), custom_call_target="tpu_custom_call" | custom-call | bytes 4718592 | tf_op jit(solution)/shard_map/prepare/pallas_call | solution.py:119
  79.3 2.5 %prepare.2.refs_8_ = bf16[3072,384]{1,0:T(8,128)(2,1)S(1)} custom-call(s32[8]{0:T(128)S(1)} %and_select_fusion.at_ref, bf16[384,1536]{1,0:T(8,128)(2,1)S(1)} %collective-permute-done.7.refs_0_, bf16[384,1536]{1,0:T(8,128)(2,1)} %collective-permute-done.8.refs_1_), custom_call_target="tpu_custom_call" | custom-call | bytes 4718592 | tf_op jit(solution)/shard_map/prepare/pallas_call | solution.py:119
  82.3 1.6 %collective-permute-start.23 = (bf16[240,384]{1,0:T(8,128)(2,1)S(1)}, bf16[240,384]{1,0:T(8,128)(2,1)S(1)}, u32[]{:S(2)}, u32[]{:S(2)}) collective-permute-start(bf16[240,384]{1,0:T(8,128)(2,1)S(1)} %copy-done.9), channel_id=1, source_target_pairs={{4,0},{8,4},{12,8},{14,12},{10,14},{6,10},{2,6},{0,2},{5,1},{9,5},... | collective-permute-start | bytes 552968 | tf_op jit(solution)/shard_map/ppermute | solution.py:301
  84.4 1.6 %collective-permute-start.16 = (bf16[312,384]{1,0:T(8,128)(2,1)S(1)}, bf16[312,384]{1,0:T(8,128)(2,1)S(1)}, u32[]{:S(2)}, u32[]{:S(2)}) collective-permute-start(bf16[312,384]{1,0:T(8,128)(2,1)S(1)} %collective-permute-done.14.refs_3_), channel_id=1, source_target_pairs={{0,4},{4,8},{8,12},{12,14},{14,10},{10,6},{6,2},{2,0},{1,5},{5,9},... | collective-permute-start | bytes 718856 | tf_op jit(solution)/shard_map/ppermute | solution.py:299
  86.4 4.0 %product.5 = (f32[384,384]{1,0:T(8,128)S(1)}, f32[384,384]{1,0:T(8,128)S(1)}) custom-call(bf16[384,384]{1,0:T(8,128)(2,1)} %get-tuple-element.17.refs_0_, bf16[384,384]{1,0:T(8,128)(2,1)} %collective-permute-done.refs_1_, bf16[384,384]{1,0:T(8,128)(2,1)} %collective-permute-done.1.refs_2_, bf16[384,384]{1,0:T(8,128)(2,1)} %collective-permute-done.2.refs_3_, ...), custom_call_target="tpu_custom_call" | custom-call | flops 1811939328 | bytes 7077888 | tf_op jit(solution)/shard_map/product/pallas_call | solution.py:149
  90.4 1.6 %collective-permute-start.11 = (f32[384,384]{1,0:T(8,128)S(1)}, f32[384,384]{1,0:T(8,128)S(1)}, u32[]{:S(2)}, u32[]{:S(2)}) collective-permute-start(f32[384,384]{1,0:T(8,128)S(1)} %get-tuple-element.21), channel_id=1, source_target_pairs={{0,1},{1,0},{2,3},{3,2},{4,5},{5,4},{6,7},{7,6},{8,9},{9,8},{10,11... | collective-permute-start | bytes 1769480 | tf_op jit(solution)/shard_map/ppermute | solution.py:308
  92.0 1.6 %collective-permute-start.30 = (bf16[192,384]{1,0:T(8,128)(2,1)S(1)}, bf16[192,384]{1,0:T(8,128)(2,1)S(1)}, u32[]{:S(2)}, u32[]{:S(2)}) collective-permute-start(bf16[192,384]{1,0:T(8,128)(2,1)S(1)} %collective-permute-done.28.refs_1_), channel_id=1, source_target_pairs={{0,4},{4,8},{8,12},{12,14},{14,10},{10,6},{6,2},{2,0},{1,5},{5,9},... | collective-permute-start | bytes 442376 | tf_op jit(solution)/shard_map/ppermute | solution.py:299
  94.7 1.5 %collective-permute-start.25 = (bf16[240,384]{1,0:T(8,128)(2,1)S(1)}, bf16[240,384]{1,0:T(8,128)(2,1)S(1)}, u32[]{:S(2)}, u32[]{:S(2)}) collective-permute-start(bf16[240,384]{1,0:T(8,128)(2,1)S(1)} %collective-permute-done.23.refs_4_), channel_id=1, source_target_pairs={{4,0},{8,4},{12,8},{14,12},{10,14},{6,10},{2,6},{0,2},{5,1},{9,5},... | collective-permute-start | bytes 552968 | tf_op jit(solution)/shard_map/ppermute | solution.py:301
  96.2 0.9 collective-permute-start.26
  97.1 3.4 %product.6 = (f32[312,384]{1,0:T(8,128)S(1)}, f32[312,384]{1,0:T(8,128)S(1)}) custom-call(bf16[312,384]{1,0:T(8,128)(2,1)} %get-tuple-element.22.refs_0_, bf16[312,384]{1,0:T(8,128)(2,1)} %collective-permute-done.12.refs_1_, bf16[312,384]{1,0:T(8,128)(2,1)} %collective-permute-done.13.refs_2_, bf16[312,384]{1,0:T(8,128)(2,1)S(1)} %collective-permute-done.14.refs_3_, ...), custom_call_target="tpu_custom_call" | custom-call | flops 1472200704 | bytes 6635520 | tf_op jit(solution)/shard_map/product/pallas_call | solution.py:149
  100.5 2.5 %collective-permute-start.19 = (f32[312,384]{1,0:T(8,128)S(1)}, f32[312,384]{1,0:T(8,128)S(1)}, u32[]{:S(2)}, u32[]{:S(2)}) collective-permute-start(f32[312,384]{1,0:T(8,128)S(1)} %get-tuple-element.24), channel_id=1, source_target_pairs={{0,1},{1,0},{2,3},{3,2},{4,5},{5,4},{6,7},{7,6},{8,9},{9,8},{10,11... | collective-permute-start | bytes 1437704 | tf_op jit(solution)/shard_map/ppermute | solution.py:308
  103.0 1.7 %collective-permute-start.32 = (bf16[192,384]{1,0:T(8,128)(2,1)S(1)}, bf16[192,384]{1,0:T(8,128)(2,1)S(1)}, u32[]{:S(2)}, u32[]{:S(2)}) collective-permute-start(bf16[192,384]{1,0:T(8,128)(2,1)S(1)} %collective-permute-done.30.refs_3_), channel_id=1, source_target_pairs={{0,4},{4,8},{8,12},{12,14},{14,10},{10,6},{6,2},{2,0},{1,5},{5,9},... | collective-permute-start | bytes 442376 | tf_op jit(solution)/shard_map/ppermute | solution.py:299
  105.0 1.7 %product.7 = (f32[240,384]{1,0:T(8,128)S(1)}, f32[240,384]{1,0:T(8,128)S(1)}) custom-call(bf16[240,384]{1,0:T(8,128)(2,1)S(1)} %copy-done.5, bf16[240,384]{1,0:T(8,128)(2,1)S(1)} %copy-done.7, bf16[240,384]{1,0:T(8,128)(2,1)S(1)} %copy-done.9, bf16[240,384]{1,0:T(8,128)(2,1)S(1)} %collective-permute-done.22.refs_3_, ...), custom_call_target="tpu_custom_call" | custom-call | flops 1132462080 | bytes 6193152 | tf_op jit(solution)/shard_map/product/pallas_call | solution.py:149
  106.9 1.2 collective-permute-done.32.refs_5_
  108.1 1.7 %collective-permute-done.34.refs_7_ = bf16[192,384]{1,0:T(8,128)(2,1)S(1)} collective-permute-done((bf16[192,384]{1,0:T(8,128)(2,1)S(1)}, bf16[192,384]{1,0:T(8,128)(2,1)S(1)}, u32[]{:S(2)}, u32[]{:S(2)}) %collective-permute-start.34) | collective-permute-done | bytes 147488 | tf_op jit(solution)/shard_map/ppermute | solution.py:301
  110.9 5.0 %collective-permute-done.19 = f32[312,384]{1,0:T(8,128)S(1)} collective-permute-done((f32[312,384]{1,0:T(8,128)S(1)}, f32[312,384]{1,0:T(8,128)S(1)}, u32[]{:S(2)}, u32[]{:S(2)}) %collective-permute-start.19) | collective-permute-done | bytes 479264 | tf_op jit(solution)/shard_map/ppermute | solution.py:308
  116.1 6.0 %collective-permute-done.27 = f32[240,384]{1,0:T(8,128)S(1)} collective-permute-done((f32[240,384]{1,0:T(8,128)S(1)}, f32[240,384]{1,0:T(8,128)S(1)}, u32[]{:S(2)}, u32[]{:S(2)}) %collective-permute-start.27) | collective-permute-done | bytes 368672 | tf_op jit(solution)/shard_map/ppermute | solution.py:308
  122.2 0.8 product.8
  123.0 2.2 %collective-permute-done.35 = f32[192,384]{1,0:T(8,128)S(1)} collective-permute-done((f32[192,384]{1,0:T(8,128)S(1)}, f32[192,384]{1,0:T(8,128)S(1)}, u32[]{:S(2)}, u32[]{:S(2)}) %collective-permute-start.35) | collective-permute-done | bytes 294944 | tf_op jit(solution)/shard_map/ppermute | solution.py:308
  125.4 1.5 %collective-permute-done.39.refs_7_ = f32[192,384]{1,0:T(8,128)S(1)} collective-permute-done((f32[192,384]{1,0:T(8,128)S(1)}, f32[192,384]{1,0:T(8,128)S(1)}, u32[]{:S(2)}, u32[]{:S(2)}) %collective-permute-start.39) | collective-permute-done | bytes 294944 | tf_op jit(solution)/shard_map/ppermute | solution.py:32
  126.9 7.2 %mirror.1 = f32[1128,384]{1,0:T(8,128)} custom-call(s32[1128]{0:T(1024)S(1)} %add_select_fusion.index_ref, f32[384,384]{1,0:T(8,128)S(1)} %add.56.refs_0_, f32[312,384]{1,0:T(8,128)S(1)} %add.57.refs_1_, f32[240,384]{1,0:T(8,128)S(1)} %add.58.refs_2_, f32[192,384]{1,0:T(8,128)S(1)} %add.59.refs_3_, f32[384,384]{1,0:T(8,128)S(1)} %collective-permute-done.36.refs_4_, ...), custom_call_target="tpu_custom_call" | custom-call | flops 433152 | bytes 5197824 | tf_op jit(solution)/shard_map/mirror/pallas_call | solution.py:221
  (84 shorter events, 8.8 us)
Async XLA Ops:
  0.0 46.6 %copy-start.14 = (s32[8]{0:T(128)S(1)}, s32[8]{0:T(128)}, u32[]{:S(2)}) copy-start(s32[8]{0:T(128)} %constant.104) | copy-start | bytes 100
  0.0 7.8 %copy-start = (bf16[1128,384]{1,0:T(8,128)(2,1)S(1)}, bf16[1128,384]{1,0:T(8,128)(2,1)}, u32[]{:S(2)}) copy-start(bf16[1128,384]{1,0:T(8,128)(2,1)} %a_ref.1) | copy-start | bytes 2598916
  4.7 29.0 %collective-permute-start.7 = (bf16[384,1536]{1,0:T(8,128)(2,1)S(1)}, bf16[384,1536]{1,0:T(8,128)(2,1)S(1)}, u32[]{:S(2)}, u32[]{:S(2)}) collective-permute-start(bf16[384,1536]{1,0:T(8,128)(2,1)S(1)} %get-tuple-element.18), channel_id=1, source_target_pairs={{0,1},{1,0},{2,3},{3,2},{4,5},{5,4},{6,7},{7,6},{8,9},{9,8},{10,11... | collective-permute-start | bytes 3538952 | tf_op jit(solution)/shard_map/ppermute | solution.py:277
  8.6 6.7 %collective-permute-start.28 = (bf16[192,384]{1,0:T(8,128)(2,1)S(1)}, bf16[192,384]{1,0:T(8,128)(2,1)S(1)}, u32[]{:S(2)}, u32[]{:S(2)}) collective-permute-start(bf16[192,384]{1,0:T(8,128)(2,1)S(1)} %get-tuple-element.28.refs_0_), channel_id=1, source_target_pairs={{0,4},{4,8},{8,12},{12,14},{14,10},{10,6},{6,2},{2,0},{1,5},{5,9},... | collective-permute-start | bytes 442376 | tf_op jit(solution)/shard_map/ppermute | solution.py:299
  10.2 26.1 %collective-permute-start.12 = (bf16[312,384]{1,0:T(8,128)(2,1)}, bf16[312,384]{1,0:T(8,128)(2,1)}, u32[]{:S(2)}, u32[]{:S(2)}) collective-permute-start(bf16[312,384]{1,0:T(8,128)(2,1)} %get-tuple-element.22.refs_0_), channel_id=1, source_target_pairs={{0,4},{4,8},{8,12},{12,14},{14,10},{10,6},{6,2},{2,0},{1,5},{5,9},... | collective-permute-start | bytes 718856 | tf_op jit(solution)/shard_map/ppermute | solution.py:299
  11.8 21.9 %collective-permute-start.20 = (bf16[240,384]{1,0:T(8,128)(2,1)S(1)}, bf16[240,384]{1,0:T(8,128)(2,1)S(1)}, u32[]{:S(2)}, u32[]{:S(2)}) collective-permute-start(bf16[240,384]{1,0:T(8,128)(2,1)S(1)} %get-tuple-element.25.refs_0_), channel_id=1, source_target_pairs={{0,4},{4,8},{8,12},{12,14},{14,10},{10,6},{6,2},{2,0},{1,5},{5,9},... | collective-permute-start | bytes 552968 | tf_op jit(solution)/shard_map/ppermute | solution.py:299
  13.4 6.4 %collective-permute-start.29 = (bf16[192,384]{1,0:T(8,128)(2,1)S(1)}, bf16[192,384]{1,0:T(8,128)(2,1)S(1)}, u32[]{:S(2)}, u32[]{:S(2)}) collective-permute-start(bf16[192,384]{1,0:T(8,128)(2,1)S(1)} %get-tuple-element.28.refs_0_), channel_id=1, source_target_pairs={{4,0},{8,4},{12,8},{14,12},{10,14},{6,10},{2,6},{0,2},{5,1},{9,5},... | collective-permute-start | bytes 442376 | tf_op jit(solution)/shard_map/ppermute | solution.py:301
  15.4 20.3 %collective-permute-start.21 = (bf16[240,384]{1,0:T(8,128)(2,1)S(1)}, bf16[240,384]{1,0:T(8,128)(2,1)S(1)}, u32[]{:S(2)}, u32[]{:S(2)}) collective-permute-start(bf16[240,384]{1,0:T(8,128)(2,1)S(1)} %get-tuple-element.25.refs_0_), channel_id=1, source_target_pairs={{4,0},{8,4},{12,8},{14,12},{10,14},{6,10},{2,6},{0,2},{5,1},{9,5},... | collective-permute-start | bytes 552968 | tf_op jit(solution)/shard_map/ppermute | solution.py:301
  19.8 15.8 %copy-start.2 = (bf16[192,384]{1,0:T(8,128)(2,1)}, bf16[192,384]{1,0:T(8,128)(2,1)S(1)}, u32[]{:S(2)}) copy-start(bf16[192,384]{1,0:T(8,128)(2,1)S(1)} %collective-permute-done.29.refs_2_) | copy-start | bytes 442372
  19.8 49.6 %collective-permute-start.9 = (bf16[384,1536]{1,0:T(8,128)(2,1)S(1)}, bf16[384,1536]{1,0:T(8,128)(2,1)}, u32[]{:S(2)}, u32[]{:S(2)}) collective-permute-start(bf16[384,1536]{1,0:T(8,128)(2,1)S(1)} %get-tuple-element.19.refs_0_), channel_id=1, source_target_pairs={{0,16},{16,0},{1,17},{17,1},{2,18},{18,2},{3,19},{19,3},{4,20},{20... | collective-permute-start | bytes 3538952 | tf_op jit(solution)/shard_map/ppermute | solution.py:32
  33.7 36.1 %collective-permute-start.8 = (bf16[384,1536]{1,0:T(8,128)(2,1)S(1)}, bf16[384,1536]{1,0:T(8,128)(2,1)}, u32[]{:S(2)}, u32[]{:S(2)}) collective-permute-start(bf16[384,1536]{1,0:T(8,128)(2,1)S(1)} %collective-permute-done.7.refs_0_), channel_id=1, source_target_pairs={{0,16},{16,0},{1,17},{17,1},{2,18},{18,2},{3,19},{19,3},{4,20},{20... | collective-permute-start | bytes 3538952 | tf_op jit(solution)/shard_map/ppermute | solution.py:32
  33.7 11.7 %collective-permute-start = (bf16[384,384]{1,0:T(8,128)(2,1)}, bf16[384,384]{1,0:T(8,128)(2,1)}, u32[]{:S(2)}, u32[]{:S(2)}) collective-permute-start(bf16[384,384]{1,0:T(8,128)(2,1)} %get-tuple-element.17.refs_0_), channel_id=1, source_target_pairs={{0,4},{4,8},{8,12},{12,14},{14,10},{10,6},{6,2},{2,0},{1,5},{5,9},... | collective-permute-start | bytes 884744 | tf_op jit(solution)/shard_map/ppermute | solution.py:299
  35.6 19.6 %collective-permute-start.10 = (bf16[1128,384]{1,0:T(8,128)(2,1)S(1)}, bf16[1128,384]{1,0:T(8,128)(2,1)}, u32[]{:S(2)}, u32[]{:S(2)}) collective-permute-start(bf16[1128,384]{1,0:T(8,128)(2,1)S(1)} %copy-done), channel_id=1, source_target_pairs={{0,16},{16,0},{1,17},{17,1},{2,18},{18,2},{3,19},{19,3},{4,20},{20... | collective-permute-start | bytes 2598920 | tf_op jit(solution)/shard_map/ppermute | solution.py:32
  36.3 8.2 %collective-permute-start.13 = (bf16[312,384]{1,0:T(8,128)(2,1)}, bf16[312,384]{1,0:T(8,128)(2,1)}, u32[]{:S(2)}, u32[]{:S(2)}) collective-permute-start(bf16[312,384]{1,0:T(8,128)(2,1)} %get-tuple-element.22.refs_0_), channel_id=1, source_target_pairs={{4,0},{8,4},{12,8},{14,12},{10,14},{6,10},{2,6},{0,2},{5,1},{9,5},... | collective-permute-start | bytes 718856 | tf_op jit(solution)/shard_map/ppermute | solution.py:301
  44.5 8.5 %collective-permute-start.1 = (bf16[384,384]{1,0:T(8,128)(2,1)}, bf16[384,384]{1,0:T(8,128)(2,1)}, u32[]{:S(2)}, u32[]{:S(2)}) collective-permute-start(bf16[384,384]{1,0:T(8,128)(2,1)} %get-tuple-element.17.refs_0_), channel_id=1, source_target_pairs={{4,0},{8,4},{12,8},{14,12},{10,14},{6,10},{2,6},{0,2},{5,1},{9,5},... | collective-permute-start | bytes 884744 | tf_op jit(solution)/shard_map/ppermute | solution.py:301
  45.4 8.9 %collective-permute-start.2 = (bf16[384,384]{1,0:T(8,128)(2,1)}, bf16[384,384]{1,0:T(8,128)(2,1)}, u32[]{:S(2)}, u32[]{:S(2)}) collective-permute-start(bf16[384,384]{1,0:T(8,128)(2,1)} %collective-permute-done.refs_1_), channel_id=1, source_target_pairs={{0,4},{4,8},{8,12},{12,14},{14,10},{10,6},{6,2},{2,0},{1,5},{5,9},... | collective-permute-start | bytes 884744 | tf_op jit(solution)/shard_map/ppermute | solution.py:299
  46.6 8.5 %copy-start.11 = (s32[1128,2]{0,1:T(2,128)S(1)}, s32[1128,2]{0,1:T(2,128)}, u32[]{:S(2)}) copy-start(s32[1128,2]{0,1:T(2,128)} %param.13) | copy-start | bytes 27076
  46.6 8.5 %copy-start.13 = (f32[48]{0:T(128)S(1)}, f32[48]{0:T(128)}, u32[]{:S(2)}) copy-start(f32[48]{0:T(128)} %param.12) | copy-start | bytes 580
  53.1 14.3 %collective-permute-start.3 = (bf16[384,384]{1,0:T(8,128)(2,1)}, bf16[384,384]{1,0:T(8,128)(2,1)}, u32[]{:S(2)}, u32[]{:S(2)}) collective-permute-start(bf16[384,384]{1,0:T(8,128)(2,1)} %collective-permute-done.1.refs_2_), channel_id=1, source_target_pairs={{4,0},{8,4},{12,8},{14,12},{10,14},{6,10},{2,6},{0,2},{5,1},{9,5},... | collective-permute-start | bytes 884744 | tf_op jit(solution)/shard_map/ppermute | solution.py:301
  54.3 14.6 %collective-permute-start.4 = (bf16[384,384]{1,0:T(8,128)(2,1)}, bf16[384,384]{1,0:T(8,128)(2,1)}, u32[]{:S(2)}, u32[]{:S(2)}) collective-permute-start(bf16[384,384]{1,0:T(8,128)(2,1)} %collective-permute-done.2.refs_3_), channel_id=1, source_target_pairs={{0,4},{4,8},{8,12},{12,14},{14,10},{10,6},{6,2},{2,0},{1,5},{5,9},... | collective-permute-start | bytes 884744 | tf_op jit(solution)/shard_map/ppermute | solution.py:299
  55.2 10.5 %copy-start.7 = (bf16[240,384]{1,0:T(8,128)(2,1)S(1)}, bf16[240,384]{1,0:T(8,128)(2,1)}, u32[]{:S(2)}) copy-start(bf16[240,384]{1,0:T(8,128)(2,1)} %copy-done.6) | copy-start | bytes 552964
  55.3 10.5 %collective-permute-start.15 = (bf16[312,384]{1,0:T(8,128)(2,1)}, bf16[312,384]{1,0:T(8,128)(2,1)S(1)}, u32[]{:S(2)}, u32[]{:S(2)}) collective-permute-start(bf16[312,384]{1,0:T(8,128)(2,1)} %collective-permute-done.13.refs_2_), channel_id=1, source_target_pairs={{4,0},{8,4},{12,8},{14,12},{10,14},{6,10},{2,6},{0,2},{5,1},{9,5},... | collective-permute-start | bytes 718856 | tf_op jit(solution)/shard_map/ppermute | solution.py:301
  65.8 16.0 %collective-permute-start.22 = (bf16[240,384]{1,0:T(8,128)(2,1)S(1)}, bf16[240,384]{1,0:T(8,128)(2,1)S(1)}, u32[]{:S(2)}, u32[]{:S(2)}) collective-permute-start(bf16[240,384]{1,0:T(8,128)(2,1)S(1)} %copy-done.7), channel_id=1, source_target_pairs={{0,4},{4,8},{8,12},{12,14},{14,10},{10,6},{6,2},{2,0},{1,5},{5,9},... | collective-permute-start | bytes 552968 | tf_op jit(solution)/shard_map/ppermute | solution.py:299
  67.4 15.0 %collective-permute-start.14 = (bf16[312,384]{1,0:T(8,128)(2,1)}, bf16[312,384]{1,0:T(8,128)(2,1)S(1)}, u32[]{:S(2)}, u32[]{:S(2)}) collective-permute-start(bf16[312,384]{1,0:T(8,128)(2,1)} %collective-permute-done.12.refs_1_), channel_id=1, source_target_pairs={{0,4},{4,8},{8,12},{12,14},{14,10},{10,6},{6,2},{2,0},{1,5},{5,9},... | collective-permute-start | bytes 718856 | tf_op jit(solution)/shard_map/ppermute | solution.py:299
  68.9 15.0 %collective-permute-start.17 = (bf16[312,384]{1,0:T(8,128)(2,1)S(1)}, bf16[312,384]{1,0:T(8,128)(2,1)S(1)}, u32[]{:S(2)}, u32[]{:S(2)}) collective-permute-start(bf16[312,384]{1,0:T(8,128)(2,1)S(1)} %collective-permute-done.15.refs_4_), channel_id=1, source_target_pairs={{4,0},{8,4},{12,8},{14,12},{10,14},{6,10},{2,6},{0,2},{5,1},{9,5},... | collective-permute-start | bytes 718856 | tf_op jit(solution)/shard_map/ppermute | solution.py:301
  69.4 15.0 %collective-permute-start.5 = (bf16[384,384]{1,0:T(8,128)(2,1)}, bf16[384,384]{1,0:T(8,128)(2,1)S(1)}, u32[]{:S(2)}, u32[]{:S(2)}) collective-permute-start(bf16[384,384]{1,0:T(8,128)(2,1)} %collective-permute-done.3.refs_4_), channel_id=1, source_target_pairs={{4,0},{8,4},{12,8},{14,12},{10,14},{6,10},{2,6},{0,2},{5,1},{9,5},... | collective-permute-start | bytes 884744 | tf_op jit(solution)/shard_map/ppermute | solution.py:301
  69.9 16.1 %collective-permute-start.6 = (bf16[384,384]{1,0:T(8,128)(2,1)}, bf16[384,384]{1,0:T(8,128)(2,1)S(1)}, u32[]{:S(2)}, u32[]{:S(2)}) collective-permute-start(bf16[384,384]{1,0:T(8,128)(2,1)} %collective-permute-done.4.refs_5_), channel_id=1, source_target_pairs={{0,4},{4,8},{8,12},{12,14},{14,10},{10,6},{6,2},{2,0},{1,5},{5,9},... | collective-permute-start | bytes 884744 | tf_op jit(solution)/shard_map/ppermute | solution.py:299
  81.8 8.6 %collective-permute-start.31 = (bf16[192,384]{1,0:T(8,128)(2,1)S(1)}, bf16[192,384]{1,0:T(8,128)(2,1)S(1)}, u32[]{:S(2)}, u32[]{:S(2)}) collective-permute-start(bf16[192,384]{1,0:T(8,128)(2,1)S(1)} %copy-done.3), channel_id=1, source_target_pairs={{4,0},{8,4},{12,8},{14,12},{10,14},{6,10},{2,6},{0,2},{5,1},{9,5},... | collective-permute-start | bytes 442376 | tf_op jit(solution)/shard_map/ppermute | solution.py:301
  82.3 9.7 %collective-permute-start.23 = (bf16[240,384]{1,0:T(8,128)(2,1)S(1)}, bf16[240,384]{1,0:T(8,128)(2,1)S(1)}, u32[]{:S(2)}, u32[]{:S(2)}) collective-permute-start(bf16[240,384]{1,0:T(8,128)(2,1)S(1)} %copy-done.9), channel_id=1, source_target_pairs={{4,0},{8,4},{12,8},{14,12},{10,14},{6,10},{2,6},{0,2},{5,1},{9,5},... | collective-permute-start | bytes 552968 | tf_op jit(solution)/shard_map/ppermute | solution.py:301
  83.9 9.7 %collective-permute-start.24 = (bf16[240,384]{1,0:T(8,128)(2,1)S(1)}, bf16[240,384]{1,0:T(8,128)(2,1)S(1)}, u32[]{:S(2)}, u32[]{:S(2)}) collective-permute-start(bf16[240,384]{1,0:T(8,128)(2,1)S(1)} %collective-permute-done.22.refs_3_), channel_id=1, source_target_pairs={{0,4},{4,8},{8,12},{12,14},{14,10},{10,6},{6,2},{2,0},{1,5},{5,9},... | collective-permute-start | bytes 552968 | tf_op jit(solution)/shard_map/ppermute | solution.py:299
  84.4 10.3 %collective-permute-start.16 = (bf16[312,384]{1,0:T(8,128)(2,1)S(1)}, bf16[312,384]{1,0:T(8,128)(2,1)S(1)}, u32[]{:S(2)}, u32[]{:S(2)}) collective-permute-start(bf16[312,384]{1,0:T(8,128)(2,1)S(1)} %collective-permute-done.14.refs_3_), channel_id=1, source_target_pairs={{0,4},{4,8},{8,12},{12,14},{14,10},{10,6},{6,2},{2,0},{1,5},{5,9},... | collective-permute-start | bytes 718856 | tf_op jit(solution)/shard_map/ppermute | solution.py:299
  85.9 10.2 %collective-permute-start.18 = (bf16[312,384]{1,0:T(8,128)(2,1)S(1)}, bf16[312,384]{1,0:T(8,128)(2,1)S(1)}, u32[]{:S(2)}, u32[]{:S(2)}) collective-permute-start(bf16[312,384]{1,0:T(8,128)(2,1)S(1)} %collective-permute-done.17.refs_6_), channel_id=1, source_target_pairs={{4,0},{8,4},{12,8},{14,12},{10,14},{6,10},{2,6},{0,2},{5,1},{9,5},... | collective-permute-start | bytes 718856 | tf_op jit(solution)/shard_map/ppermute | solution.py:301
  90.4 14.6 %copy-start.5 = (bf16[240,384]{1,0:T(8,128)(2,1)S(1)}, bf16[240,384]{1,0:T(8,128)(2,1)}, u32[]{:S(2)}) copy-start(bf16[240,384]{1,0:T(8,128)(2,1)} %copy-done.4) | copy-start | bytes 552964
  90.4 20.3 %collective-permute-start.11 = (f32[384,384]{1,0:T(8,128)S(1)}, f32[384,384]{1,0:T(8,128)S(1)}, u32[]{:S(2)}, u32[]{:S(2)}) collective-permute-start(f32[384,384]{1,0:T(8,128)S(1)} %get-tuple-element.21), channel_id=1, source_target_pairs={{0,1},{1,0},{2,3},{3,2},{4,5},{5,4},{6,7},{7,6},{8,9},{9,8},{10,11... | collective-permute-start | bytes 1769480 | tf_op jit(solution)/shard_map/ppermute | solution.py:308
  92.0 8.5 %collective-permute-start.30 = (bf16[192,384]{1,0:T(8,128)(2,1)S(1)}, bf16[192,384]{1,0:T(8,128)(2,1)S(1)}, u32[]{:S(2)}, u32[]{:S(2)}) collective-permute-start(bf16[192,384]{1,0:T(8,128)(2,1)S(1)} %collective-permute-done.28.refs_1_), channel_id=1, source_target_pairs={{0,4},{4,8},{8,12},{12,14},{14,10},{10,6},{6,2},{2,0},{1,5},{5,9},... | collective-permute-start | bytes 442376 | tf_op jit(solution)/shard_map/ppermute | solution.py:299
  93.6 9.4 %collective-permute-start.33 = (bf16[192,384]{1,0:T(8,128)(2,1)S(1)}, bf16[192,384]{1,0:T(8,128)(2,1)S(1)}, u32[]{:S(2)}, u32[]{:S(2)}) collective-permute-start(bf16[192,384]{1,0:T(8,128)(2,1)S(1)} %collective-permute-done.31.refs_4_), channel_id=1, source_target_pairs={{4,0},{8,4},{12,8},{14,12},{10,14},{6,10},{2,6},{0,2},{5,1},{9,5},... | collective-permute-start | bytes 442376 | tf_op jit(solution)/shard_map/ppermute | solution.py:301
  94.7 10.0 %collective-permute-start.25 = (bf16[240,384]{1,0:T(8,128)(2,1)S(1)}, bf16[240,384]{1,0:T(8,128)(2,1)S(1)}, u32[]{:S(2)}, u32[]{:S(2)}) collective-permute-start(bf16[240,384]{1,0:T(8,128)(2,1)S(1)} %collective-permute-done.23.refs_4_), channel_id=1, source_target_pairs={{4,0},{8,4},{12,8},{14,12},{10,14},{6,10},{2,6},{0,2},{5,1},{9,5},... | collective-permute-start | bytes 552968 | tf_op jit(solution)/shard_map/ppermute | solution.py:301
  96.2 8.9 %collective-permute-start.26 = (bf16[240,384]{1,0:T(8,128)(2,1)S(1)}, bf16[240,384]{1,0:T(8,128)(2,1)S(1)}, u32[]{:S(2)}, u32[]{:S(2)}) collective-permute-start(bf16[240,384]{1,0:T(8,128)(2,1)S(1)} %collective-permute-done.24.refs_5_), channel_id=1, source_target_pairs={{0,4},{4,8},{8,12},{12,14},{14,10},{10,6},{6,2},{2,0},{1,5},{5,9},... | collective-permute-start | bytes 552968 | tf_op jit(solution)/shard_map/ppermute | solution.py:299
  100.5 15.5 %collective-permute-start.19 = (f32[312,384]{1,0:T(8,128)S(1)}, f32[312,384]{1,0:T(8,128)S(1)}, u32[]{:S(2)}, u32[]{:S(2)}) collective-permute-start(f32[312,384]{1,0:T(8,128)S(1)} %get-tuple-element.24), channel_id=1, source_target_pairs={{0,1},{1,0},{2,3},{3,2},{4,5},{5,4},{6,7},{7,6},{8,9},{9,8},{10,11... | collective-permute-start | bytes 1437704 | tf_op jit(solution)/shard_map/ppermute | solution.py:308
  103.0 5.1 %collective-permute-start.32 = (bf16[192,384]{1,0:T(8,128)(2,1)S(1)}, bf16[192,384]{1,0:T(8,128)(2,1)S(1)}, u32[]{:S(2)}, u32[]{:S(2)}) collective-permute-start(bf16[192,384]{1,0:T(8,128)(2,1)S(1)} %collective-permute-done.30.refs_3_), channel_id=1, source_target_pairs={{0,4},{4,8},{8,12},{12,14},{14,10},{10,6},{6,2},{2,0},{1,5},{5,9},... | collective-permute-start | bytes 442376 | tf_op jit(solution)/shard_map/ppermute | solution.py:299
  104.7 5.1 %collective-permute-start.34 = (bf16[192,384]{1,0:T(8,128)(2,1)S(1)}, bf16[192,384]{1,0:T(8,128)(2,1)S(1)}, u32[]{:S(2)}, u32[]{:S(2)}) collective-permute-start(bf16[192,384]{1,0:T(8,128)(2,1)S(1)} %collective-permute-done.33.refs_6_), channel_id=1, source_target_pairs={{4,0},{8,4},{12,8},{14,12},{10,14},{6,10},{2,6},{0,2},{5,1},{9,5},... | collective-permute-start | bytes 442376 | tf_op jit(solution)/shard_map/ppermute | solution.py:301
  106.8 15.3 %collective-permute-start.27 = (f32[240,384]{1,0:T(8,128)S(1)}, f32[240,384]{1,0:T(8,128)S(1)}, u32[]{:S(2)}, u32[]{:S(2)}) collective-permute-start(f32[240,384]{1,0:T(8,128)S(1)} %get-tuple-element.27), channel_id=1, source_target_pairs={{0,1},{1,0},{2,3},{3,2},{4,5},{5,4},{6,7},{7,6},{8,9},{9,8},{10,11... | collective-permute-start | bytes 1105928 | tf_op jit(solution)/shard_map/ppermute | solution.py:308
  110.6 14.6 %collective-permute-start.35 = (f32[192,384]{1,0:T(8,128)S(1)}, f32[192,384]{1,0:T(8,128)S(1)}, u32[]{:S(2)}, u32[]{:S(2)}) collective-permute-start(f32[192,384]{1,0:T(8,128)S(1)} %product.9), channel_id=1, source_target_pairs={{0,1},{1,0},{2,3},{3,2},{4,5},{5,4},{6,7},{7,6},{8,9},{9,8},{10,11... | collective-permute-start | bytes 884744 | tf_op jit(solution)/shard_map/ppermute | solution.py:308
  110.8 16.1 %collective-permute-start.36 = (f32[384,384]{1,0:T(8,128)S(1)}, f32[384,384]{1,0:T(8,128)S(1)}, u32[]{:S(2)}, u32[]{:S(2)}) collective-permute-start(f32[384,384]{1,0:T(8,128)S(1)} %add.56.refs_0_), channel_id=1, source_target_pairs={{0,16},{16,0},{1,17},{17,1},{2,18},{18,2},{3,19},{19,3},{4,20},{20... | collective-permute-start | bytes 1769480 | tf_op jit(solution)/shard_map/ppermute | solution.py:32
  116.0 10.9 %collective-permute-start.37 = (f32[312,384]{1,0:T(8,128)S(1)}, f32[312,384]{1,0:T(8,128)S(1)}, u32[]{:S(2)}, u32[]{:S(2)}) collective-permute-start(f32[312,384]{1,0:T(8,128)S(1)} %add.57.refs_1_), channel_id=1, source_target_pairs={{0,16},{16,0},{1,17},{17,1},{2,18},{18,2},{3,19},{19,3},{4,20},{20... | collective-permute-start | bytes 1437704 | tf_op jit(solution)/shard_map/ppermute | solution.py:32
  122.1 3.2 %copy-start.12 = (s32[1128]{0:T(1024)S(1)}, s32[1128]{0:T(1024)}, u32[]{:S(2)}) copy-start(s32[1128]{0:T(1024)} %param.14) | copy-start | bytes 13540
  122.1 4.8 %collective-permute-start.38 = (f32[240,384]{1,0:T(8,128)S(1)}, f32[240,384]{1,0:T(8,128)S(1)}, u32[]{:S(2)}, u32[]{:S(2)}) collective-permute-start(f32[240,384]{1,0:T(8,128)S(1)} %add.58.refs_2_), channel_id=1, source_target_pairs={{0,16},{16,0},{1,17},{17,1},{2,18},{18,2},{3,19},{19,3},{4,20},{20... | collective-permute-start | bytes 1105928 | tf_op jit(solution)/shard_map/ppermute | solution.py:32
  125.3 1.6 %collective-permute-start.39 = (f32[192,384]{1,0:T(8,128)S(1)}, f32[192,384]{1,0:T(8,128)S(1)}, u32[]{:S(2)}, u32[]{:S(2)}) collective-permute-start(f32[192,384]{1,0:T(8,128)S(1)} %add.59.refs_3_), channel_id=1, source_target_pairs={{0,16},{16,0},{1,17},{17,1},{2,18},{18,2},{3,19},{19,3},{4,20},{20... | collective-permute-start | bytes 884744 | tf_op jit(solution)/shard_map/ppermute | solution.py:32
  (7 other events, 11.3 us)
